TPU v7x, 256 devices: a whole 4x4x8 slice. The times are simulated.
256 devices in a mesh: rows: 32 (over z, x), cols: 8 (over y, core).
Axes of the slice: x: 4, y: 4, z: 8, core: 2. Of those that a mesh axis runs over, the one named last changes fastest.
Arguments:
- features: bfloat16 [524288, 440], P(('rows', 'cols')), may hold values from -12 to 12
- residual: float32 [524288, 147], P(('rows', 'cols')), may hold values from -6 to 6
- coeffs: float32 [524288, 147], P(('rows', 'cols')), may hold values from -3 to 3
- block_inverse: float32 [2, 2048, 2048], P(None, ('rows', 'cols')), may hold values from -0.0234375 to 0.0234375
- block_index: int32 [2, 2048], P(None, 'cols'), may hold values from 0 to 2047, as said below
- owners: int32 [2], replicated, may hold values from 0 to 31
Outputs:
- new_coeffs: float32 [524288, 147], P(('rows', 'cols'))
- new_residual: float32 [524288, 147], P(('rows', 'cols'))
Inputs may be any that keep to these rules, and one draw needn't show every extreme that they name: `block_index`: for each step and each aligned run of 256 positions, the indices are distinct.
All inputs are finite; a program needn't handle non-finite values.
Results may differ from a plain program's by a relative error of at most 0.0028.
Values may be sent and summed in bfloat16 or wider, within the bound.
A program may use at most 64 MiB of HBM per device.

v0:
```python
import jax
import jax.numpy as jnp
from jax import lax
from jax.sharding import Mesh
from jax.sharding import PartitionSpec as P

ROWS = ("rows_0", "rows_1")
COLS = ("cols_0", "cols_1")
ROWS_COLS = ("rows_0", "rows_1", "cols_0", "cols_1")


penalty = 0.5


def from_root(value, axes, root):
    value = jnp.where(lax.axis_index(axes) == root, value, jnp.zeros_like(value))
    for axis in axes:
        value = lax.psum(value, axis)
    return value


def in_order(parts, dim):
    shape = list(parts.shape[1:])
    shape[dim] *= parts.shape[0]
    return jnp.moveaxis(parts, 0, dim).reshape(shape)


def copy_for_each(value, axis):
    copies = jnp.broadcast_to(value, (lax.axis_size(axis), *value.shape))
    return lax.all_to_all(copies, axis, split_axis=0, concat_axis=0, tiled=True)


def collect(value, axis, dim):
    return in_order(copy_for_each(value, axis), dim)


def from_root_2(value, axis, root):
    return lax.dynamic_index_in_dim(lax.all_gather(value, axis), root, 0, keepdims=False)


def stacked_from(value, axes, order):
    parts = value[None]
    for k in order:
        parts = lax.all_gather(parts, axes[k], axis=0, tiled=True)
    block = [lax.axis_size(axes[k]) for k in reversed(order)]
    parts = parts.reshape(*block, *value.shape)
    turned = sorted(range(len(order)), key=lambda place: order[len(order) - 1 - place])
    return parts.transpose(*turned, *range(len(order), parts.ndim)).reshape(-1, *value.shape)


def gather_axes(value, axes, order, dim):
    return in_order(stacked_from(value, axes, order), dim)


def per_device(features, residual, coeffs, block_inverse, block_index, owners):
    frame_count = features.shape[0]
    feature_width = features.shape[1]
    per_col = block_index.shape[1]
    row_block = min(512, frame_count)
    exponent = -1.0 / feature_width
    my_row = lax.axis_index(ROWS)
    my_col = lax.axis_index(COLS)
    squares = jnp.sum(jnp.square(features.astype(jnp.float32)), axis=1)
    feature_blocks = features.reshape(frame_count // row_block, row_block, feature_width)
    norm_blocks = squares.reshape(frame_count // row_block, row_block)
    for step_id in range(block_index.shape[0]):
        chosen_rows = block_index[step_id]
        owner_row = owners[step_id]
        mine_feat = jnp.take(features, chosen_rows, axis=0)
        mine_res = jnp.take(residual, chosen_rows, axis=0)
        row_piece = from_root(mine_feat, ROWS, owner_row)
        chosen = collect(row_piece, COLS, 0)
        res_piece = from_root_2(mine_res, ROWS, owner_row)
        picked_res = collect(res_piece, COLS, 0)
        my_update = jnp.dot(
            block_inverse[step_id],
            picked_res,
            precision=lax.Precision.HIGHEST,
            preferred_element_type=jnp.float32,
        ).astype(jnp.bfloat16)
        update = gather_axes(my_update, ROWS_COLS, (1, 0, 2, 3), 0)
        chosen_norms = jnp.sum(jnp.square(chosen.astype(jnp.float32)), axis=1)

        def kernel_rows(operands):
            block_rows, block_norms = operands
            inner = lax.dot_general(
                block_rows, chosen, (((1,), (1,)), ((), ())), preferred_element_type=jnp.float32
            )
            distance = block_norms[:, None] + chosen_norms[None, :] - 2.0 * inner
            kernel = jnp.exp(distance * exponent).astype(jnp.bfloat16)
            return jnp.dot(kernel, update, preferred_element_type=jnp.float32)

        change = lax.map(kernel_rows, (feature_blocks, norm_blocks)).reshape(frame_count, -1)
        residual = residual - change
        is_owner = jnp.where(my_row == owner_row, 1.0, 0.0).astype(jnp.float32)
        mine_update = (
            lax.dynamic_slice_in_dim(update, my_col * per_col, per_col, 0).astype(jnp.float32)
            * is_owner
        )
        residual = residual.at[chosen_rows].add(-penalty * mine_update)
        coeffs = coeffs.at[chosen_rows].add(mine_update)
    return (coeffs, residual)


def solution(mesh):
    split = Mesh(mesh.devices.reshape(8, 4, 4, 2), ("rows_0", "rows_1", "cols_0", "cols_1"))
    in_specs = (
        P(ROWS_COLS, None),
        P(ROWS_COLS, None),
        P(ROWS_COLS, None),
        P(None, ROWS_COLS, None),
        P(None, COLS),
        P(),
    )
    out_specs = (P(ROWS_COLS, None), P(ROWS_COLS, None))
    return jax.shard_map(
        per_device, mesh=split, in_specs=in_specs, out_specs=out_specs, check_vma=False
    )
```

profile of v0, /device:TPU:1, one launch (start us, length us, event | category | flops | bytes accessed | tf_op | source)
XLA Modules:
  0.0 525.2 jit_solution(5898855721030536369)
XLA Ops:
  8.8 1.4 fusion.41
  11.5 2.8 copy.53
  14.3 1.9 gather_fusion.1
  16.2 1.9 gather_fusion.3
  18.0 1.8 select_select_fusion.1
  19.8 1.8 select_select_fusion
  21.6 72.7 %all-reduce.5.cloned.1.call-done = (bf16[256,440]{1,0:T(8,128)(2,1)}, bf16[256,440]{1,0:T(8,128)(2,1)}) async-done(((bf16[256,440]{1,0:T(8,128)(2,1)}, bf16[256,440]{1,0:T(8,128)(2,1)}), (bf16[256,440]{1,0:T(8,128)(2,1)}, bf16[256,440]{1,0:T(8,128)(2,1)})) %all-reduce.5.cloned.1.call-update) | async-done | bytes 450576 | tf_op jit(solution)/shard_map/psum | solution.py:18
  95.3 1.0 gather_fusion
  97.1 49.7 %all-reduce.7.cloned.1.call-done = (bf16[256,440]{1,0:T(8,128)(2,1)}, bf16[256,440]{1,0:T(8,128)(2,1)}) async-done(((bf16[256,440]{1,0:T(8,128)(2,1)}, bf16[256,440]{1,0:T(8,128)(2,1)}), (bf16[256,440]{1,0:T(8,128)(2,1)}, bf16[256,440]{1,0:T(8,128)(2,1)})) %all-reduce.7.cloned.1.call-update) | async-done | bytes 450576 | tf_op jit(solution)/shard_map/psum | solution.py:18
  146.7 1.1 copy.54
  147.8 1.4 broadcast_in_dim.53
  149.2 7.2 %all-to-all-start.1 = ((bf16[8,256,440]{1,2,0:T(8,128)(2,1)}), bf16[8,256,440]{1,2,0:T(8,128)(2,1)S(1)}, u32[]{:S(2)}, u32[]{:S(2)}) async-start(bf16[8,256,440]{1,2,0:T(8,128)(2,1)} %broadcast_in_dim.53), calls=%async_computation.1 | async-start | bytes 3604480 | tf_op jit(solution)/shard_map/all_to_all | solution.py:30
  158.1 40.6 %all-gather.7.cloned.1.call-done = f32[8192,147]{1,0:T(8,128)} async-done(((f32[256,147]{1,0:T(8,128)}), f32[8192,147]{1,0:T(8,128)}) %all-gather.7.cloned.1.call-update) | async-done | bytes 4816912 | tf_op jit(solution)/shard_map/all_gather | solution.py:38
  198.7 1.0 constant_dynamic-slice_fusion.3
  199.8 1.1 broadcast_in_dim.51
  200.9 5.9 %all-to-all-start = ((f32[8,256,147]{1,2,0:T(8,128)}), f32[8,256,147]{1,2,0:T(8,128)S(1)}, u32[]{:S(2)}, u32[]{:S(2)}) async-start(f32[8,256,147]{1,2,0:T(8,128)} %broadcast_in_dim.51), calls=%async_computation | async-start | bytes 2490368 | tf_op jit(solution)/shard_map/all_to_all | solution.py:30
  206.8 1.9 multiply_reduce_fusion.2
  209.1 2.7 copy.72
  211.8 12.0 %all-to-all-done = f32[8,256,147]{1,2,0:T(8,128)S(1)} async-done(((f32[8,256,147]{1,2,0:T(8,128)}), f32[8,256,147]{1,2,0:T(8,128)S(1)}, u32[]{:S(2)}, u32[]{:S(2)}) %all-to-all-start) | async-done | bytes 1204256 | tf_op jit(solution)/shard_map/all_to_all | solution.py:30
  225.1 1.1 fusion.18
  226.2 9.1 %all-gather.1 = bf16[32,147]{1,0:T(8,128)(2,1)S(1)} all-gather(bf16[8,147]{1,0:T(8,128)(2,1)S(1)} %fusion.18), channel_id=3, replica_groups=mesh['rows_0'=8,'rows_1'=4,'cols_0'=4,'cols_1'=2] {'rows_1'}, dimensions={0}, use_global_device_ids=true | all-gather | bytes 11760 | tf_op jit(solution)/shard_map/all_gather | solution.py:44
  235.3 18.3 %all_gather.39 = bf16[32,8,147]{2,1,0:T(8,128)(2,1)S(1)} all-gather(bf16[4,8,147]{2,1,0:T(8,128)(2,1)S(1)} %bitcast.119), channel_id=1, replica_groups=mesh['rows_0'=8,'rows_1'=4,'cols_0'=4,'cols_1'=2] {'rows_0'}, dimensions={0}, use_global_device_ids=true | all-gather | bytes 84672 | tf_op jit(solution)/shard_map/all_gather | solution.py:44
  253.6 9.9 %all_gather.40 = bf16[128,8,147]{2,1,0:T(8,128)(2,1)S(1)} all-gather(bf16[32,8,147]{2,1,0:T(8,128)(2,1)S(1)} %all_gather.39), channel_id=1, replica_groups=mesh['rows_0'=8,'rows_1'=4,'cols_0'=4,'cols_1'=2] {'cols_0'}, dimensions={0}, use_global_device_ids=true | all-gather | bytes 376320 | tf_op jit(solution)/shard_map/all_gather | solution.py:44
  264.0 14.9 %all_gather.41 = bf16[256,8,147]{0,1,2:T(8,128)(2,1)S(1)} all-gather(bf16[128,8,147]{0,1,2:T(8,128)(2,1)S(1)} %copy.49), channel_id=1, replica_groups=mesh['rows_0'=8,'rows_1'=4,'cols_0'=4,'cols_1'=2] {'cols_1'}, dimensions={0}, use_global_device_ids=true | all-gather | bytes 903168 | tf_op jit(solution)/shard_map/all_gather | solution.py:44
  278.9 1.0 copy.50
  280.0 1.1 copy.51
  281.9 14.0 %while.20 = (s32[]{:T(128)}, f32[4,512,147]{1,2,0:T(8,128)S(1)}, f32[4,512]{1,0:T(4,128)S(1)}, f32[2048]{0:T(1024)S(1)}, bf16[4,512,440]{2,1,0:T(8,128)(2,1)}, /...) while((s32[]{:T(128)}, f32[4,512,147]{1,2,0:T(8,128)S(1)}, f32[4,512]{1,0:T(4,128)S(1)}, ...), condition=%wide.region_6.9_spmd, body=%wide.region_5.8_spmd.sunk | while | flops 1236271104 | bytes 3996769 | solution.py:93
  282.0 3.5 fusion.59
  285.5 3.5 fusion.59
  289.0 3.5 fusion.59
  292.5 3.5 fusion.59
  296.0 1.8 copy.58
  297.8 2.5 bitcast_subtract_fusion.1
  300.3 3.3 scatter_custom_fusion.1
  303.6 1.0 gather_fusion.2
  305.5 1.4 broadcast_in_dim.56
  306.9 4.6 all-to-all-start.3
  313.6 84.1 %all-gather.9.cloned.1.call-done = f32[8192,147]{1,0:T(8,128)} async-done(((f32[256,147]{1,0:T(8,128)}), f32[8192,147]{1,0:T(8,128)}) %all-gather.9.cloned.1.call-update) | async-done | bytes 4816912 | tf_op jit(solution)/shard_map/all_gather | solution.py:38
  397.7 1.0 constant_dynamic-slice_fusion.2
  398.8 1.1 broadcast_in_dim.54
  399.9 5.8 %all-to-all-start.2 = ((f32[8,256,147]{1,2,0:T(8,128)}), f32[8,256,147]{1,2,0:T(8,128)S(1)}, u32[]{:S(2)}, u32[]{:S(2)}) async-start(f32[8,256,147]{1,2,0:T(8,128)} %broadcast_in_dim.54), calls=%async_computation.2 | async-start | bytes 2490368 | tf_op jit(solution)/shard_map/all_to_all | solution.py:30
  405.6 2.8 copy.52
  408.4 1.9 multiply_reduce_fusion
  410.3 3.8 copy.73
  414.1 5.1 scatter_custom_fusion
  419.1 3.6 all-to-all-done.2
  423.6 1.1 fusion.19
  424.7 9.1 %all-gather.3 = bf16[32,147]{1,0:T(8,128)(2,1)S(1)} all-gather(bf16[8,147]{1,0:T(8,128)(2,1)S(1)} %fusion.19), channel_id=5, replica_groups=mesh['rows_0'=8,'rows_1'=4,'cols_0'=4,'cols_1'=2] {'rows_1'}, dimensions={0}, use_global_device_ids=true | all-gather | bytes 11760 | tf_op jit(solution)/shard_map/all_gather | solution.py:44
  433.8 18.3 %all_gather.45 = bf16[32,8,147]{2,1,0:T(8,128)(2,1)S(1)} all-gather(bf16[4,8,147]{2,1,0:T(8,128)(2,1)S(1)} %bitcast.120), channel_id=1, replica_groups=mesh['rows_0'=8,'rows_1'=4,'cols_0'=4,'cols_1'=2] {'rows_0'}, dimensions={0}, use_global_device_ids=true | all-gather | bytes 84672 | tf_op jit(solution)/shard_map/all_gather | solution.py:44
  452.1 9.9 %all_gather.46 = bf16[128,8,147]{2,1,0:T(8,128)(2,1)S(1)} all-gather(bf16[32,8,147]{2,1,0:T(8,128)(2,1)S(1)} %all_gather.45), channel_id=1, replica_groups=mesh['rows_0'=8,'rows_1'=4,'cols_0'=4,'cols_1'=2] {'cols_0'}, dimensions={0}, use_global_device_ids=true | all-gather | bytes 376320 | tf_op jit(solution)/shard_map/all_gather | solution.py:44
  462.5 15.1 %all_gather.47 = bf16[256,8,147]{0,1,2:T(8,128)(2,1)} all-gather(bf16[128,8,147]{0,1,2:T(8,128)(2,1)S(1)} %copy.62), channel_id=1, replica_groups=mesh['rows_0'=8,'rows_1'=4,'cols_0'=4,'cols_1'=2] {'cols_1'}, dimensions={0}, use_global_device_ids=true | all-gather | bytes 903168 | tf_op jit(solution)/shard_map/all_gather | solution.py:44
  477.6 1.9 copy.63
  479.5 1.1 copy.64
  480.6 5.1 scatter_custom_fusion.2
  485.6 2.7 copy.70
  488.4 16.6 %while.21 = (s32[]{:T(128)}, f32[4,512,147]{1,2,0:T(8,128)S(1)}, f32[4,512]{1,0:T(4,128)S(1)}, f32[2048]{0:T(1024)S(1)}, bf16[4,512,440]{2,1,0:T(8,128)(2,1)}, /...) while((s32[]{:T(128)}, f32[4,512,147]{1,2,0:T(8,128)S(1)}, f32[4,512]{1,0:T(4,128)S(1)}, ...), condition=%wide.region_13.16_spmd, body=%wide.region_12.15_spmd.sunk | while | flops 1236271104 | bytes 3996769 | solution.py:93
  488.5 4.1 fusion.63
  492.6 4.1 fusion.63
  496.8 4.1 fusion.63
  500.9 4.1 fusion.63
  505.0 1.8 copy.69
  506.8 3.2 bitcast_subtract_fusion
  510.0 5.1 scatter_custom_fusion.3
  515.1 2.7 copy.71
  (58 shorter events, 8.4 us)
Async XLA Ops:
  8.0 86.4 %all-reduce.5.cloned.1.call-start = ((), (), s32[]{:S(2)}) async-start(), calls=%async_computation.6 | async-start | bytes 1048576 | tf_op jit(solution)/shard_map/psum | solution.py:18
  14.3 3.7 copy-start.1
  16.2 78.3 %copy-start.3 = (f32[2048,147]{0,1:T(8,128)S(1)}, f32[2048,147]{0,1:T(8,128)}, u32[]{:S(2)}) copy-start(f32[2048,147]{0,1:T(8,128)} %param.15) | copy-start | bytes 3612676
  21.6 125.2 %all-reduce.7.cloned.1.call-start = ((), (), s32[]{:S(2)}) async-start(), calls=%async_computation.7 | async-start | bytes 1048576 | tf_op jit(solution)/shard_map/psum | solution.py:18
  94.4 104.3 %all-gather.7.cloned.1.call-start = ((), (), s32[]{:S(2)}) async-start(), calls=%async_computation.4 | async-start | bytes 8650752 | tf_op jit(solution)/shard_map/all_gather | solution.py:38
  95.3 53.9 %copy-start = (f32[2048,147]{1,0:T(8,128)}, f32[2048,147]{1,0:T(8,128)S(1)}, u32[]{:S(2)}) copy-start(f32[2048,147]{1,0:T(8,128)S(1)} %copy.46) | copy-start | bytes 3612676
  149.2 50.6 %all-to-all-start.1 = ((bf16[8,256,440]{1,2,0:T(8,128)(2,1)}), bf16[8,256,440]{1,2,0:T(8,128)(2,1)S(1)}, u32[]{:S(2)}, u32[]{:S(2)}) async-start(bf16[8,256,440]{1,2,0:T(8,128)(2,1)} %broadcast_in_dim.53), calls=%async_computation.1 | async-start | bytes 3604480 | tf_op jit(solution)/shard_map/all_to_all | solution.py:30
  200.9 7.8 %copy-start.6 = (s32[2,256]{1,0:T(2,128)S(1)}, s32[2,256]{1,0:T(2,128)}, u32[]{:S(2)}) copy-start(s32[2,256]{1,0:T(2,128)} %param.18) | copy-start | bytes 6148
  200.9 23.0 %all-to-all-start = ((f32[8,256,147]{1,2,0:T(8,128)}), f32[8,256,147]{1,2,0:T(8,128)S(1)}, u32[]{:S(2)}, u32[]{:S(2)}) async-start(f32[8,256,147]{1,2,0:T(8,128)} %broadcast_in_dim.51), calls=%async_computation | async-start | bytes 2490368 | tf_op jit(solution)/shard_map/all_to_all | solution.py:30
  206.8 190.9 %all-gather.9.cloned.1.call-start = ((), (), s32[]{:S(2)}) async-start(), calls=%async_computation.5 | async-start | bytes 8650752 | tf_op jit(solution)/shard_map/all_gather | solution.py:38
  224.2 0.9 copy-start.5
  280.0 2.0 copy-start.2
  303.6 1.8 copy-start.4
  306.9 91.8 %all-to-all-start.3 = ((bf16[8,256,440]{1,2,0:T(8,128)(2,1)}), bf16[8,256,440]{1,2,0:T(8,128)(2,1)}, u32[]{:S(2)}, u32[]{:S(2)}) async-start(bf16[8,256,440]{1,2,0:T(8,128)(2,1)} %broadcast_in_dim.56), calls=%async_computation.3 | async-start | bytes 3604480 | tf_op jit(solution)/shard_map/all_to_all | solution.py:30
  399.9 22.8 %all-to-all-start.2 = ((f32[8,256,147]{1,2,0:T(8,128)}), f32[8,256,147]{1,2,0:T(8,128)S(1)}, u32[]{:S(2)}, u32[]{:S(2)}) async-start(f32[8,256,147]{1,2,0:T(8,128)} %broadcast_in_dim.54), calls=%async_computation.2 | async-start | bytes 2490368 | tf_op jit(solution)/shard_map/all_to_all | solution.py:30
Sparse Core Ops, SparseCore 0:
  21.7 72.6 all-reduce.4
  96.8 49.8 all-reduce.6
Sparse Core Ops, SparseCore 1:
  98.0 100.6 all-gather.6
  305.5 92.2 all-gather.8
where the time goes:
time: 527 us; the launch traced here: 525 us
  waiting for transfers between devices  263 us (50%)
  blocking collectives  105 us (20%)
  local copies, waits for them, and re-layouts  47.4 us (9%)
  other arithmetic  33.4 us (6%)
  matrix products  32.5 us (6%)
  starting transfers between devices  23.5 us (4%)
  between operations  20.9 us (4%)
    all_gather x2, waiting for transfers between devices, from_root_2(): lax.all_gather(value, axis)  125 us
    psum x2, waiting for transfers between devices, from_root(): value = lax.psum(value, axis)  122 us
    all_gather x8, blocking collectives, stacked_from(): parts = lax.all_gather(parts, axes[k], axis=0, tiled=True)  105 us
    dot_general x8, matrix products, kernel_rows(): return jnp.dot(kernel, update, preferred_element_type=jnp.float32)  30.4 us
    all_to_all x4, starting transfers between devices, copy_for_each(): return lax.all_to_all(copies, axis, split_axis=0, concat_axis=0, tiled=True)  23.4 us
    all_to_all x4, waiting for transfers between devices, copy_for_each(): return lax.all_to_all(copies, axis, split_axis=0, concat_axis=0, tiled=True)  15.6 us
    unnamed x27, local copies, waits for them, and re-layouts  14.1 us
  transfers between devices with their start and end apart: 8, of which 6 were waited for; matrix products, arithmetic and copies ran while one was open for 5% of the time, Pallas kernels for 0%

commit v1 on v0

v1 whole, which is shorter than its diff:
```python
import functools
import math

import jax
import jax.numpy as jnp
from jax import lax
from jax.experimental import pallas as pl
from jax.experimental.pallas import tpu as pltpu
from jax.sharding import PartitionSpec as P

MESH = pl.DeviceIdType.MESH
NZ, NX, NY, NK = 8, 4, 4, 2
PICK = 256
BLOCK = 2048
PAD_D = 512
PAD_C = 256
TILE = 256
F32 = jnp.float32
BF16 = jnp.bfloat16

STAGES = {
    "r_rsx": 4, "r_rsz": 8, "r_agz": 8, "r_agx": 4,
    "y_rsx": 8, "y_rsz": 8, "y_agz": 8, "y_ag2": 4, "y_ag3": 16, "y_core": 16,
    "p": 8, "u_agz": 8, "u_ag2": 4, "u_ag3": 16, "u_core": 16,
}
BASE = {}
_total = 0
for _name, _count in STAGES.items():
    BASE[_name] = _total
    _total += 2 * _count
BASE["b"] = _total
N_SEMS = _total + 8


def split3(value):
    hi = value.astype(BF16)
    rest = value - hi.astype(F32)
    mid = rest.astype(BF16)
    lo = (rest - mid.astype(F32)).astype(BF16)
    return hi.astype(F32), mid.astype(F32), lo.astype(F32)


def dot_t(a, b):
    return lax.dot_general(a, b, (((1,), (1,)), ((), ())), preferred_element_type=F32)


def with_norms(tail, squares, parts_at, ones_at, axis=1):
    lane = lax.broadcasted_iota(jnp.int32, tail.shape, axis)
    hi, mid, lo = split3(-0.5 * squares)
    out = jnp.where(lane < 56, tail, 0.0)
    out = jnp.where((lane >= ones_at) & (lane < ones_at + 3), 1.0, out)
    out = jnp.where(lane == parts_at, hi, out)
    out = jnp.where(lane == parts_at + 1, mid, out)
    return jnp.where(lane == parts_at + 2, lo, out)


def body(width, outs, owners, feat, res, binv, idxr, chg, dco,
         idxc, xa, cho, rcho, rrx0, rrx1, rsel, rrz0, rrz1, rch, rbuf, rx0, rx1, sel, rz0, rz1, ych,
         ybuf, bg, pbuf, up, uch, ubuf, ut, kb, k21, ssem, rsem, lsem):
    rrx, rrz, rx, rz = (rrx0, rrx1), (rrz0, rrz1), (rx0, rx1), (rz0, rz1)
    r = lax.axis_index("rows")
    c = lax.axis_index("cols")
    z, x = r // NX, r % NX
    y, k = c // NK, c % NK
    scale = 2.0 / width * math.log2(math.e)
    khalf = pl.ds(pl.multiple_of(k * 256, 256), 256)
    klane = pl.ds(pl.multiple_of(k * 128, 128), 128)
    tail_start = 384
    tail_used = width - tail_start

    def dev(zz, xx, yy, kk):
        return (zz * NX + xx, yy * NK + kk)

    desc = {}

    def send(name, s, i, src, dst, target):
        at = BASE[name] + (s * STAGES[name] + i if name in STAGES else i)
        copy = pltpu.make_async_remote_copy(
            src_ref=src, dst_ref=dst, send_sem=ssem.at[at], recv_sem=rsem.at[at],
            device_id=target, device_id_type=MESH)
        copy.start()
        desc[(name, s, i)] = copy

    def arrived(name, s, i):
        desc[(name, s, i)].wait_recv()

    local_count = [0]

    def local(src, dst):
        copy = pltpu.make_async_copy(src, dst, lsem.at[local_count[0]])
        local_count[0] += 1
        copy.start()
        return copy

    peers = []
    for i in range(NX):
        for kk in range(NK):
            if (i, kk) != (0, 0):
                peers.append(dev(z, (x + i) % NX, y, (k + kk) % NK))
    for i in range(1, NZ):
        peers.append(dev((z + i) % NZ, x, y, k))
    for i in range(1, NY):
        for kk in range(NK):
            peers.append(dev(z, x, (y + i) % NY, (k + kk) % NK))
    barrier = pltpu.get_barrier_semaphore()
    for peer in peers:
        pl.semaphore_signal(barrier, inc=1, device_id=peer, device_id_type=MESH)

    rcho[...] = jnp.zeros_like(rcho)
    res_hi = res[...].astype(BF16)
    res_lo = (res[...] - res_hi.astype(F32)).astype(BF16)
    diagonal = (lax.broadcasted_iota(jnp.int32, (PICK, PICK), 0)
                == lax.broadcasted_iota(jnp.int32, (PICK, PICK), 1))

    def chosen_at(s):
        index = jnp.broadcast_to(idxr[s:s + 1, :], (PICK, PICK))
        return jnp.sum(jnp.where(diagonal, index, 0).astype(F32), axis=1,
                       keepdims=True).astype(jnp.int32)

    def picks(s, start, size):
        position = lax.broadcasted_iota(jnp.int32, (PICK, size), 1) + start
        return jnp.where(idxc[s] == position, 1.0, 0.0)

    for s in range(2):
        idxc[s] = chosen_at(s)
        pick = picks(s, 0, BLOCK).astype(BF16)
        rcho[s, :, 0:outs] = dot_t(pick, res_hi) + dot_t(pick, res_lo)
        rows = dot_t(pick, feat[...])
        squares = jnp.sum(rows * rows, axis=1, keepdims=True)
        cho[s, :, 0:width] = rows.astype(BF16)
        cho[s, :, tail_start:PAD_D] = with_norms(
            cho[s, :, tail_start:PAD_D].astype(F32), squares, tail_used + 3, tail_used).astype(BF16)

    pl.semaphore_wait(barrier, len(peers))

    waits = {}

    def r_rsx(s):
        for i in range(1, NX):
            xx = (x + i) % NX
            send("r_rsx", s, i, rcho.at[s, pl.ds(pl.multiple_of(xx * 64, 64), 64), :],
                 rrx[s].at[x], dev(z, xx, y, k))
        waits[("r_rsx", s)] = local(
            rcho.at[s, pl.ds(pl.multiple_of(x * 64, 64), 64), :], rrx[s].at[x])

    def y_rsx(s):
        for i in range(NX):
            xx = (x + i) % NX
            for kk in range(NK):
                if (i, kk) == (0, 0):
                    continue
                k2 = (k + kk) % NK
                send("y_rsx", s, i * NK + kk,
                     cho.at[s, pl.ds(pl.multiple_of(xx * 64, 64), 64),
                            pl.ds(pl.multiple_of(k2 * 256, 256), 256)],
                     rx[s].at[x, k], dev(z, xx, y, k2))
        waits[("y_rsx", s)] = local(
            cho.at[s, pl.ds(pl.multiple_of(x * 64, 64), 64), khalf], rx[s].at[x, k])

    def r_rsz(s):
        for i in range(1, NX):
            arrived("r_rsx", s, i)
        waits[("r_rsx", s)].wait()
        rsel[s] = rrx[s][owners[s] % NX]
        for i in range(NZ):
            zz = (z + i) % NZ
            src = rsel.at[s, pl.ds(pl.multiple_of(zz * 8, 8), 8), :]
            if i == 0:
                waits[("r_rsz", s)] = local(src, rrz[s].at[z])
            else:
                send("r_rsz", s, i, src, rrz[s].at[z], dev(zz, x, y, k))

    def y_rsz(s):
        for i in range(NX):
            for kk in range(NK):
                if (i, kk) != (0, 0):
                    arrived("y_rsx", s, i * NK + kk)
        waits[("y_rsx", s)].wait()
        sel[s] = rx[s][owners[s] % NX]
        for i in range(NZ):
            zz = (z + i) % NZ
            src = sel.at[s, zz // 4, pl.ds(pl.multiple_of((zz % 4) * 16, 16), 16), :]
            if i == 0:
                waits[("y_rsz", s)] = local(src, rz[s].at[z])
            else:
                send("y_rsz", s, i, src, rz[s].at[z], dev(zz, x, y, k))

    def r_agz(s):
        for i in range(1, NZ):
            arrived("r_rsz", s, i)
        waits[("r_rsz", s)].wait()
        rch[s] = rrz[s][owners[s] // NX]
        place = rbuf.at[s, pl.ds(pl.multiple_of(x * 64 + z * 8, 8), 8), :]
        for i in range(1, NZ):
            send("r_agz", s, i, rch.at[s], place, dev((z + i) % NZ, x, y, k))
        waits[("r_agz", s)] = local(rch.at[s], place)

    def y_agz(s):
        for i in range(1, NZ):
            arrived("y_rsz", s, i)
        waits[("y_rsz", s)].wait()
        ych[s] = rz[s][owners[s] // NX]
        place = ybuf.at[s, 2 * y + z // 4, x,
                        pl.ds(pl.multiple_of((z % 4) * 16, 16), 16), khalf]
        for i in range(1, NZ):
            send("y_agz", s, i, ych.at[s], place, dev((z + i) % NZ, x, y, k))
        waits[("y_agz", s)] = local(ych.at[s], place)

    def r_agx(s):
        for i in range(1, NZ):
            arrived("r_agz", s, i)
        waits[("r_agz", s)].wait()
        part = rbuf.at[s, pl.ds(pl.multiple_of(x * 64, 64), 64), :]
        for i in range(1, NX):
            send("r_agx", s, i, part, part, dev(z, (x + i) % NX, y, k))

    g = (1 - k) * x + k * y
    q = (1 - k) * y + k * x

    def y_block(s, gg, qq):
        bx = (1 - k) * gg + k * qq
        by = k * gg + (1 - k) * qq
        return ybuf.at[s, pl.ds(2 * by, 2), bx, :, khalf]

    def u_block(s, gg, qq):
        bx = (1 - k) * gg + k * qq
        by = k * gg + (1 - k) * qq
        return ubuf.at[s, :, bx, by, :, klane]

    def to_second(i):
        return dev(z, (x + i * (1 - k)) % NX, (y + i * k) % NY, k)

    def to_third(i):
        return dev(z, (x + i * k) % NX, (y + i * (1 - k)) % NY, k)

    def ring_send(kind, block, s, d):
        part = block(s, (g - d + NX) % NX, q)
        for i in range(1, NY):
            send(kind + "_ag3", s, d * 4 + i, part, part, to_third(i))
        send(kind + "_core", s, d * 4, part, part, dev(z, x, y, 1 - k))

    def ag2_start(kind, block, s):
        for i in range(1, NZ):
            arrived(kind + "_agz", s, i)
        waits[(kind + "_agz", s)].wait()
        part = block(s, g, q)
        for i in range(1, NX):
            send(kind + "_ag2", s, i, part, part, to_second(i))
        ring_send(kind, block, s, 0)

    def ag3_start(kind, block, s):
        for d in range(1, NX):
            arrived(kind + "_ag2", s, d)
            ring_send(kind, block, s, d)

    def core_start(kind, block, s):
        for d in range(NX):
            for i in range(1, NY):
                arrived(kind + "_ag3", s, d * 4 + i)
                part = block(s, (g - d + NX) % NX, (q - i + NY) % NY)
                send(kind + "_core", s, d * 4 + i, part, part, dev(z, x, y, 1 - k))

    def core_end(kind, s):
        for d in range(NX):
            for i in range(NY):
                arrived(kind + "_core", s, d * 4 + i)

    def partial_start(s, values):
        pbuf[s] = jnp.dot(bg[s], values, precision=lax.Precision.HIGHEST,
                          preferred_element_type=F32)
        for i in range(NY * NK):
            cc = (c + i) % (NY * NK)
            src = pbuf.at[s, pl.ds(pl.multiple_of((cc // NK) * 16, 16), 16),
                          pl.ds(pl.multiple_of((cc % NK) * 128, 128), 128)]
            if i == 0:
                waits[("p", s)] = local(src, up.at[s, c])
            else:
                send("p", s, i, src, up.at[s, c], (r, cc))

    def u_agz(s):
        for i in range(1, NY * NK):
            arrived("p", s, i)
        waits[("p", s)].wait()
        uch[s] = jnp.sum(up[s], axis=0).astype(BF16)
        place = ubuf.at[s, z, x, y, :, klane]
        for i in range(1, NZ):
            send("u_agz", s, i, uch.at[s], place, dev((z + i) % NZ, x, y, k))
        waits[("u_agz", s)] = local(uch.at[s], place)

    def gen(s, first, last):
        @pl.loop(first, last)
        def _(t):
            at = pl.ds(pl.multiple_of(t * TILE, TILE), TILE)
            points = ybuf[s, t].reshape(TILE, PAD_D)
            for j in range(4):
                inner = jnp.dot(points, xa[:, j * 512:(j + 1) * 512], preferred_element_type=F32)
                kb[s, at, j * 512:(j + 1) * 512] = jnp.exp2(inner * scale).astype(BF16)

    def turn(s):
        ut[s] = jnp.transpose(ubuf[s].reshape(BLOCK, PAD_C))

    r_rsx(0)
    y_rsx(0)
    for i in range(NY * NK):
        cc = (c + i) % (NY * NK)
        src = binv.at[:, :, pl.ds(pl.multiple_of(cc * PICK, PICK), PICK)]
        dst = bg.at[:, pl.ds(pl.multiple_of(c * 8, 8), 8), :]
        if i == 0:
            waits["b"] = local(src, dst)
        else:
            send("b", 0, i, src, dst, (r, cc))
    r_rsx(1)
    y_rsx(1)

    xa[0:width, :] = feat[...]

    @pl.loop(0, BLOCK // TILE)
    def _(t):
        at = pl.ds(pl.multiple_of(t * TILE, TILE), TILE)
        rows = feat[:, at].astype(F32)
        squares = jnp.sum(rows * rows, axis=0, keepdims=True)
        xa[tail_start:PAD_D, at] = with_norms(
            xa[tail_start:PAD_D, at].astype(F32), squares, tail_used, tail_used + 3, 0).astype(BF16)

    r_rsz(0)
    y_rsz(0)
    r_rsz(1)
    y_rsz(1)
    r_agz(0)
    y_agz(0)
    r_agz(1)
    y_agz(1)
    r_agx(0)
    ag2_start("y", y_block, 0)
    for i in range(1, NX):
        arrived("r_agx", 0, i)
    for i in range(1, NY * NK):
        arrived("b", 0, i)
    waits["b"].wait()
    partial_start(0, rbuf[0])
    r_agx(1)
    ag2_start("y", y_block, 1)
    ag3_start("y", y_block, 0)
    u_agz(0)
    ag3_start("y", y_block, 1)
    core_start("y", y_block, 0)
    core_end("y", 0)
    gen(0, 0, 2)
    ag2_start("u", u_block, 0)
    gen(0, 2, 4)
    ag3_start("u", u_block, 0)
    core_start("y", y_block, 1)
    gen(0, 4, 6)
    core_start("u", u_block, 0)
    gen(0, 6, 8)
    core_end("y", 1)

    second = ybuf[1, c].reshape(PICK, PAD_D)
    tail = second[:, tail_start:PAD_D].astype(F32)
    lane = lax.broadcasted_iota(jnp.int32, tail.shape, 1)
    turned = pltpu.roll(tail, 125, 1)
    tail = jnp.where((lane >= tail_used) & (lane < tail_used + 3), turned, tail)
    tail = jnp.where((lane >= tail_used + 3) & (lane < tail_used + 6), 1.0, tail)
    second = jnp.concatenate([second[:, :tail_start], tail.astype(BF16)], axis=1)
    for j in range(4):
        inner = dot_t(second, ybuf[0, 2 * j:2 * j + 2].reshape(512, PAD_D))
        k21[:, j * 512:(j + 1) * 512] = jnp.exp2(inner * scale).astype(BF16)
    for i in range(1, NX):
        arrived("r_agx", 1, i)

    core_end("u", 0)
    turn(0)
    moved = jnp.dot(k21[...], ubuf[0].reshape(BLOCK, PAD_C), preferred_element_type=F32)
    same = jnp.where(owners[0] == owners[1], 0.5, 0.0).astype(F32)
    twice = jnp.where(idxc[1] == idxr[0:1, :], same, 0.0).astype(BF16)
    moved += jnp.dot(twice, ubuf[0, c].reshape(PICK, PAD_C), preferred_element_type=F32)
    partial_start(1, rbuf[1] - moved)
    gen(1, 0, 2)
    u_agz(1)
    gen(1, 2, 4)
    ag2_start("u", u_block, 1)
    gen(1, 4, 6)
    ag3_start("u", u_block, 1)
    gen(1, 6, 8)
    core_start("u", u_block, 1)
    core_end("u", 1)

    turn(1)
    own = [jnp.where(owners[s] == r, 1.0, 0.0).astype(F32) for s in range(2)]
    mine = [ut[s, :, pl.ds(pl.multiple_of(c * PICK, PICK), PICK)] for s in range(2)]

    @pl.loop(0, BLOCK // 512)
    def _(t):
        at = pl.ds(pl.multiple_of(t * 512, 512), 512)
        change = jnp.dot(ut[0], kb[0, :, at], preferred_element_type=F32)
        change += jnp.dot(ut[1], kb[1, :, at], preferred_element_type=F32)
        added = jnp.zeros((PAD_C, 512), F32)
        for s in range(2):
            put = (picks(s, t * 512, 512) * own[s]).astype(BF16)
            added += jnp.dot(mine[s], put, preferred_element_type=F32)
        chg[:, at] = (change + 0.5 * added)[:outs, :]
        dco[:, at] = added[:outs, :]

    for copy in desc.values():
        copy.wait_send()


def per_device(features, residual, coeffs, block_inverse, block_index, owners):
    frames, width = features.shape
    outs = residual.shape[1]
    vmem = pl.BlockSpec(memory_space=pltpu.VMEM)
    change, added = pl.pallas_call(
        functools.partial(body, width, outs),
        out_shape=(jax.ShapeDtypeStruct((outs, frames), F32),
                   jax.ShapeDtypeStruct((outs, frames), F32)),
        in_specs=[pl.BlockSpec(memory_space=pltpu.SMEM)] + [vmem] * 4,
        out_specs=(vmem, vmem),
        scratch_shapes=[
            pltpu.VMEM((2, PICK, 1), jnp.int32),
            pltpu.VMEM((PAD_D, BLOCK), BF16),
            pltpu.VMEM((2, PICK, PAD_D), BF16),
            pltpu.VMEM((2, PICK, PAD_C), F32),
            pltpu.VMEM((NX, 64, PAD_C), F32),
            pltpu.VMEM((NX, 64, PAD_C), F32),
            pltpu.VMEM((2, 64, PAD_C), F32),
            pltpu.VMEM((NZ, 8, PAD_C), F32),
            pltpu.VMEM((NZ, 8, PAD_C), F32),
            pltpu.VMEM((2, 8, PAD_C), F32),
            pltpu.VMEM((2, PICK, PAD_C), F32),
            pltpu.VMEM((NX, NK, 64, 256), BF16),
            pltpu.VMEM((NX, NK, 64, 256), BF16),
            pltpu.VMEM((2, NK, 64, 256), BF16),
            pltpu.VMEM((NZ, 16, 256), BF16),
            pltpu.VMEM((NZ, 16, 256), BF16),
            pltpu.VMEM((2, 16, 256), BF16),
            pltpu.VMEM((2, 8, NX, 64, PAD_D), BF16),
            pltpu.VMEM((2, 64, PICK), F32),
            pltpu.VMEM((2, 64, PAD_C), F32),
            pltpu.VMEM((2, 8, 16, 128), F32),
            pltpu.VMEM((2, 16, 128), BF16),
            pltpu.VMEM((2, NZ, NX, NY, 16, PAD_C), BF16),
            pltpu.VMEM((2, PAD_C, BLOCK), BF16),
            pltpu.VMEM((2, BLOCK, BLOCK), BF16),
            pltpu.VMEM((PICK, BLOCK), BF16),
            pltpu.SemaphoreType.DMA((N_SEMS,)),
            pltpu.SemaphoreType.DMA((N_SEMS,)),
            pltpu.SemaphoreType.DMA((24,)),
        ],
        compiler_params=pltpu.CompilerParams(
            collective_id=0, has_side_effects=True, vmem_limit_bytes=60 * 1024 * 1024),
        name="steps",
    )(owners, features.T, residual.T, block_inverse, block_index)
    return coeffs + added.T, residual - change.T


def solution(mesh):
    both = ("rows", "cols")
    in_specs = (P(both, None), P(both, None), P(both, None), P(None, both, None),
                P(None, "cols"), P())
    out_specs = (P(both, None), P(both, None))
    return jax.shard_map(per_device, mesh=mesh, in_specs=in_specs, out_specs=out_specs,
                         check_vma=False)
```

time: 527 us -> 101 us (0.19)
  waiting for transfers between devices: 263 us -> 0 us
  blocking collectives: 105 us -> 0 us
  Pallas kernels: 0 us -> 97 us
  local copies, waits for them, and re-layouts: 47.4 us -> 0.01 us
  matrix products: 32.5 us -> 0 us
  other arithmetic: 33.4 us -> 3.57 us
  starting transfers between devices: 23.5 us -> 0 us
  between operations: 20.9 us -> 0.67 us
    all_gather x2 -> x0, waiting for transfers between devices: 125 us -> none  [from_root_2(): lax.all_gather(value, axis)]
    psum x2 -> x0, waiting for transfers between devices: 122 us -> none  [from_root(): value = lax.psum(value, axis)]
    all_gather x8 -> x0, blocking collectives: 105 us -> none  [stacked_from(): parts = lax.all_gather(parts, axes[k], axis=0, tiled=True)]
    pallas_call x0 -> x1, Pallas kernels: none -> 97 us  [per_device(): pl.pallas_call(functools.partial(body, width, outs), out_shape=(jax.Shape...]
    dot_general x10 -> x0, matrix products: 32.5 us -> none  [the longest x8 30.4 us: kernel_rows(): return jnp.dot(kernel, update, preferred_element_type=jnp.float32)]
    all_to_all x4 -> x0, starting transfers between devices: 23.4 us -> none  [copy_for_each(): return lax.all_to_all(copies, axis, split_axis=0, concat_axis=0, tiled=True)]
    scatter-add x4 -> x0, other arithmetic: 18.5 us -> none  [the longest x2 10.1 us: per_device(): coeffs = coeffs.at[chosen_rows].add(mine_update)]
    all_to_all x4 -> x0, waiting for transfers between devices: 15.6 us -> none  [copy_for_each(): return lax.all_to_all(copies, axis, split_axis=0, concat_axis=0, tiled=True)]
  transfers between devices with their start and end apart: 8 -> 0, of which waited for: 6 -> 0; matrix products, arithmetic and copies ran while one was open for 5% -> 0% of each run, Pallas kernels for 0% -> 0%
where the time goes in v1:
time: 101 us
  Pallas kernels  97 us (96%)
  other arithmetic  3.57 us (4%)
    pallas_call x1, Pallas kernels, per_device(): pl.pallas_call(functools.partial(body, width, outs), out_shape=(jax.Shape...  97 us
    sub x1, other arithmetic, per_device(): return (coeffs + added.T, residual - change.T)  3.57 us

profile of v1, /device:TPU:1, one launch (start us, length us, event | category | flops | bytes accessed | tf_op | source)
XLA Modules:
  0.0 101.2 jit_solution(14015164086349923609)
XLA Ops:
  0.6 0.0 copy-start
  0.6 0.0 copy-start.1
  0.7 97.0 %steps.1 = (f32[147,2048]{1,0:T(8,128)}, f32[147,2048]{1,0:T(8,128)}) custom-call(s32[2]{0:T(128)} %owners.1, bf16[440,2048]{1,0:T(8,128)(2,1)} %bitcast.7, f32[147,2048]{1,0:T(8,128)} %bitcast.6, f32[2,8,2048]{2,1,0:T(8,128)} %binv.1, s32[2,256]{1,0:T(2,128)} %idxr.1), custom_call_target="tpu_custom_call" | custom-call | tf_op jit(solution)/shard_map/steps/pallas_call | solution.py:412
  97.6 0.0 copy-done
  97.6 0.0 copy-done.1
  97.6 3.6 %bitcast_subtract_fusion = (f32[2048,147]{0,1:T(8,128)}, f32[2048,147]{0,1:T(8,128)}) fusion(f32[2048,147]{0,1:T(8,128)S(1)} %copy-done, f32[147,2048]{1,0:T(8,128)} %get-tuple-element.5, f32[2048,147]{0,1:T(8,128)S(1)} %copy-done.1, f32[147,2048]{1,0:T(8,128)} %get-tuple-element.4), kind=kLoop, calls=%fused_computation | loop fusion | flops 602112 | bytes 7225344 | tf_op jit(solution)/shard_map/sub | solution.py:453
Async XLA Ops:
  0.6 97.0 %copy-start = (f32[2048,147]{0,1:T(8,128)S(1)}, f32[2048,147]{0,1:T(8,128)}, u32[]{:S(2)}) copy-start(f32[2048,147]{0,1:T(8,128)} %param.7) | copy-start | bytes 3612676
  0.6 97.0 %copy-start.1 = (f32[2048,147]{0,1:T(8,128)S(1)}, f32[2048,147]{0,1:T(8,128)}, u32[]{:S(2)}) copy-start(f32[2048,147]{0,1:T(8,128)} %param.8) | copy-start | bytes 3612676

commit v2 on v1

--- a/solution.py
+++ b/solution.py
@@ -54,8 +54,8 @@
     return jnp.where(lane == parts_at + 2, lo, out)
 
 
-def body(width, outs, owners, feat, res, binv, idxr, chg, dco,
-         idxc, xa, cho, rcho, rrx0, rrx1, rsel, rrz0, rrz1, rch, rbuf, rx0, rx1, sel, rz0, rz1, ych,
+def body(width, outs, owners, feat, res_in, binv_in, idxr, chg, dco,
+         idxc, res, binv, xa, cho, rcho, rrx0, rrx1, rsel, rrz0, rrz1, rch, rbuf, rx0, rx1, sel, rz0, rz1, ych,
          ybuf, bg, pbuf, up, uch, ubuf, ut, kb, k21, ssem, rsem, lsem):
     rrx, rrz, rx, rz = (rrx0, rrx1), (rrz0, rrz1), (rx0, rx1), (rz0, rz1)
     r = lax.axis_index("rows")
@@ -106,9 +106,8 @@
     for peer in peers:
         pl.semaphore_signal(barrier, inc=1, device_id=peer, device_id_type=MESH)
 
+    copies = [local(res_in, res), local(feat, xa.at[0:width, :]), local(binv_in, binv)]
     rcho[...] = jnp.zeros_like(rcho)
-    res_hi = res[...].astype(BF16)
-    res_lo = (res[...] - res_hi.astype(F32)).astype(BF16)
     diagonal = (lax.broadcasted_iota(jnp.int32, (PICK, PICK), 0)
                 == lax.broadcasted_iota(jnp.int32, (PICK, PICK), 1))
 
@@ -121,16 +120,23 @@
         position = lax.broadcasted_iota(jnp.int32, (PICK, size), 1) + start
         return jnp.where(idxc[s] == position, 1.0, 0.0)
 
-    for s in range(2):
+    def choose_res(s):
         idxc[s] = chosen_at(s)
         pick = picks(s, 0, BLOCK).astype(BF16)
+        res_hi = res[...].astype(BF16)
+        res_lo = (res[...] - res_hi.astype(F32)).astype(BF16)
         rcho[s, :, 0:outs] = dot_t(pick, res_hi) + dot_t(pick, res_lo)
-        rows = dot_t(pick, feat[...])
+
+    def choose_feat(s):
+        pick = picks(s, 0, BLOCK).astype(BF16)
+        rows = dot_t(pick, xa[0:width, :])
         squares = jnp.sum(rows * rows, axis=1, keepdims=True)
         cho[s, :, 0:width] = rows.astype(BF16)
         cho[s, :, tail_start:PAD_D] = with_norms(
             cho[s, :, tail_start:PAD_D].astype(F32), squares, tail_used + 3, tail_used).astype(BF16)
 
+    copies[0].wait()
+    choose_res(0)
     pl.semaphore_wait(barrier, len(peers))
 
     waits = {}
@@ -233,11 +239,27 @@
     def to_third(i):
         return dev(z, (x + i * k) % NX, (y + i * (1 - k)) % NY, k)
 
+    def to_core(kind, block, s, d, i):
+        part = block(s, (g - d + NX) % NX, (q - i + NY) % NY)
+        send(kind + "_core", s, d * 4 + i, part, part, dev(z, x, y, 1 - k))
+
     def ring_send(kind, block, s, d):
         part = block(s, (g - d + NX) % NX, q)
-        for i in range(1, NY):
+        for i in (1, 3):
             send(kind + "_ag3", s, d * 4 + i, part, part, to_third(i))
-        send(kind + "_core", s, d * 4, part, part, dev(z, x, y, 1 - k))
+        to_core(kind, block, s, d, 0)
+
+    def ring_pass(kind, block, s, d):
+        for i, slot, half in ((1, 2, 0), (3, 0, 1)):
+            arrived(kind + "_ag3", s, d * 4 + i)
+            part = half_of(kind, block(s, (g - d + NX) % NX, (q - i + NY) % NY), half)
+            send(kind + "_ag3", s, d * 4 + slot, part, part, to_third(i))
+            to_core(kind, block, s, d, i)
+
+    def half_of(kind, ref, half):
+        if kind == "y":
+            return ref.at[half:half + 1]
+        return ref.at[half * 4:half * 4 + 4]
 
     def ag2_start(kind, block, s):
         for i in range(1, NZ):
@@ -253,12 +275,15 @@
             arrived(kind + "_ag2", s, d)
             ring_send(kind, block, s, d)
 
+    def pass_start(kind, block, s):
+        for d in range(NX):
+            ring_pass(kind, block, s, d)
+
     def core_start(kind, block, s):
         for d in range(NX):
-            for i in range(1, NY):
-                arrived(kind + "_ag3", s, d * 4 + i)
-                part = block(s, (g - d + NX) % NX, (q - i + NY) % NY)
-                send(kind + "_core", s, d * 4 + i, part, part, dev(z, x, y, 1 - k))
+            arrived(kind + "_ag3", s, d * 4 + 2)
+            arrived(kind + "_ag3", s, d * 4)
+            to_core(kind, block, s, d, 2)
 
     def core_end(kind, s):
         for d in range(NX):
@@ -300,7 +325,7 @@
         ut[s] = jnp.transpose(ubuf[s].reshape(BLOCK, PAD_C))
 
     r_rsx(0)
-    y_rsx(0)
+    copies[2].wait()
     for i in range(NY * NK):
         cc = (c + i) % (NY * NK)
         src = binv.at[:, :, pl.ds(pl.multiple_of(cc * PICK, PICK), PICK)]
@@ -309,49 +334,55 @@
             waits["b"] = local(src, dst)
         else:
             send("b", 0, i, src, dst, (r, cc))
-    r_rsx(1)
+    copies[1].wait()
+    choose_feat(0)
+    r_rsz(0)
+    y_rsx(0)
+    choose_res(1)
+    choose_feat(1)
+    r_agz(0)
+    y_rsz(0)
     y_rsx(1)
-
-    xa[0:width, :] = feat[...]
 
     @pl.loop(0, BLOCK // TILE)
     def _(t):
         at = pl.ds(pl.multiple_of(t * TILE, TILE), TILE)
-        rows = feat[:, at].astype(F32)
+        rows = xa[0:width, at].astype(F32)
         squares = jnp.sum(rows * rows, axis=0, keepdims=True)
         xa[tail_start:PAD_D, at] = with_norms(
             xa[tail_start:PAD_D, at].astype(F32), squares, tail_used, tail_used + 3, 0).astype(BF16)
 
-    r_rsz(0)
-    y_rsz(0)
-    r_rsz(1)
-    y_rsz(1)
-    r_agz(0)
+    r_agx(0)
     y_agz(0)
-    r_agz(1)
-    y_agz(1)
-    r_agx(0)
-    ag2_start("y", y_block, 0)
+    r_rsx(1)
     for i in range(1, NX):
         arrived("r_agx", 0, i)
     for i in range(1, NY * NK):
         arrived("b", 0, i)
     waits["b"].wait()
     partial_start(0, rbuf[0])
+    ag2_start("y", y_block, 0)
+    y_rsz(1)
+    u_agz(0)
+    ag3_start("y", y_block, 0)
+    r_rsz(1)
+    y_agz(1)
+    ag2_start("u", u_block, 0)
+    pass_start("y", y_block, 0)
+    r_agz(1)
+    ag3_start("u", u_block, 0)
+    core_start("y", y_block, 0)
+    ag2_start("y", y_block, 1)
+    pass_start("u", u_block, 0)
+    core_end("y", 0)
     r_agx(1)
-    ag2_start("y", y_block, 1)
-    ag3_start("y", y_block, 0)
-    u_agz(0)
+    gen(0, 0, 2)
+    core_start("u", u_block, 0)
     ag3_start("y", y_block, 1)
-    core_start("y", y_block, 0)
-    core_end("y", 0)
-    gen(0, 0, 2)
-    ag2_start("u", u_block, 0)
     gen(0, 2, 4)
-    ag3_start("u", u_block, 0)
+    pass_start("y", y_block, 1)
+    gen(0, 4, 6)
     core_start("y", y_block, 1)
-    gen(0, 4, 6)
-    core_start("u", u_block, 0)
     gen(0, 6, 8)
     core_end("y", 1)
 
@@ -382,6 +413,7 @@
     gen(1, 4, 6)
     ag3_start("u", u_block, 1)
     gen(1, 6, 8)
+    pass_start("u", u_block, 1)
     core_start("u", u_block, 1)
     core_end("u", 1)
 
@@ -413,10 +445,12 @@
         functools.partial(body, width, outs),
         out_shape=(jax.ShapeDtypeStruct((outs, frames), F32),
                    jax.ShapeDtypeStruct((outs, frames), F32)),
-        in_specs=[pl.BlockSpec(memory_space=pltpu.SMEM)] + [vmem] * 4,
+        in_specs=[pl.BlockSpec(memory_space=pltpu.SMEM)] + [pl.BlockSpec(memory_space=pl.ANY)] * 3 + [vmem],
         out_specs=(vmem, vmem),
         scratch_shapes=[
             pltpu.VMEM((2, PICK, 1), jnp.int32),
+            pltpu.VMEM((outs, BLOCK), F32),
+            pltpu.VMEM((2, 8, BLOCK), F32),
             pltpu.VMEM((PAD_D, BLOCK), BF16),
             pltpu.VMEM((2, PICK, PAD_D), BF16),
             pltpu.VMEM((2, PICK, PAD_C), F32),

time: 101 us -> 102 us (level)
  no operation moved by 1% of the time
where the time goes in v2:
time: 102 us
  Pallas kernels  97.4 us (95%)
  other arithmetic  3.57 us (4%)
    pallas_call x1, Pallas kernels, per_device(): pl.pallas_call(functools.partial(body, width, outs), out_shape=(jax.Shape...  97.4 us
    sub x1, other arithmetic, per_device(): return (coeffs + added.T, residual - change.T)  3.57 us

profile of v2, /device:TPU:1, one launch (start us, length us, event | category | flops | bytes accessed | tf_op | source)
XLA Modules:
  0.0 101.6 jit_solution(4051981763076245223)
XLA Ops:
  0.6 0.0 copy-start
  0.6 0.0 copy-start.1
  0.7 97.4 %steps.1 = (f32[147,2048]{1,0:T(8,128)}, f32[147,2048]{1,0:T(8,128)}) custom-call(s32[2]{0:T(128)} %owners.1, bf16[440,2048]{1,0:T(8,128)(2,1)} %bitcast.7, f32[147,2048]{1,0:T(8,128)} %bitcast.6, f32[2,8,2048]{2,1,0:T(8,128)} %binv_in.1, s32[2,256]{1,0:T(2,128)} %idxr.1), custom_call_target="tpu_custom_call" | custom-call | tf_op jit(solution)/shard_map/steps/pallas_call | solution.py:444
  98.0 0.0 copy-done
  98.0 0.0 copy-done.1
  98.0 3.6 %bitcast_subtract_fusion = (f32[2048,147]{0,1:T(8,128)}, f32[2048,147]{0,1:T(8,128)}) fusion(f32[2048,147]{0,1:T(8,128)S(1)} %copy-done, f32[147,2048]{1,0:T(8,128)} %get-tuple-element.5, f32[2048,147]{0,1:T(8,128)S(1)} %copy-done.1, f32[147,2048]{1,0:T(8,128)} %get-tuple-element.4), kind=kLoop, calls=%fused_computation | loop fusion | flops 602112 | bytes 7225344 | tf_op jit(solution)/shard_map/sub | solution.py:487
Async XLA Ops:
  0.6 97.4 %copy-start = (f32[2048,147]{0,1:T(8,128)S(1)}, f32[2048,147]{0,1:T(8,128)}, u32[]{:S(2)}) copy-start(f32[2048,147]{0,1:T(8,128)} %param.7) | copy-start | bytes 3612676
  0.6 97.4 %copy-start.1 = (f32[2048,147]{0,1:T(8,128)S(1)}, f32[2048,147]{0,1:T(8,128)}, u32[]{:S(2)}) copy-start(f32[2048,147]{0,1:T(8,128)} %param.8) | copy-start | bytes 3612676

commit v3 on v2

--- a/solution.py
+++ b/solution.py
@@ -14,6 +14,7 @@
 BLOCK = 2048
 PAD_D = 512
 PAD_C = 256
+PAD_R = 160
 TILE = 256
 F32 = jnp.float32
 BF16 = jnp.bfloat16
@@ -54,8 +55,8 @@
     return jnp.where(lane == parts_at + 2, lo, out)
 
 
-def body(width, outs, owners, feat, res_in, binv_in, idxr, chg, dco,
-         idxc, res, binv, xa, cho, rcho, rrx0, rrx1, rsel, rrz0, rrz1, rch, rbuf, rx0, rx1, sel, rz0, rz1, ych,
+def body(width, outs, owners, feat, res_in, co_in, binv_in, idxr, new_co, new_res,
+         idxc, res, co, binv, xa, cho, rcho, rrx0, rrx1, rsel, rrz0, rrz1, rch, rbuf, rx0, rx1, sel, rz0, rz1, ych,
          ybuf, bg, pbuf, up, uch, ubuf, ut, kb, k21, ssem, rsem, lsem):
     rrx, rrz, rx, rz = (rrx0, rrx1), (rrz0, rrz1), (rx0, rx1), (rz0, rz1)
     r = lax.axis_index("rows")
@@ -72,24 +73,37 @@
         return (zz * NX + xx, yy * NK + kk)
 
     desc = {}
-
-    def send(name, s, i, src, dst, target):
+    sent = []
+
+    def when(need, action):
+        if need is None:
+            action()
+        else:
+            pl.when(need)(action)
+
+    def send(name, s, i, src, dst, target, need=None):
         at = BASE[name] + (s * STAGES[name] + i if name in STAGES else i)
         copy = pltpu.make_async_remote_copy(
             src_ref=src, dst_ref=dst, send_sem=ssem.at[at], recv_sem=rsem.at[at],
             device_id=target, device_id_type=MESH)
-        copy.start()
+        when(need, copy.start)
         desc[(name, s, i)] = copy
-
-    def arrived(name, s, i):
-        desc[(name, s, i)].wait_recv()
+        sent.append((copy, need))
+
+    def arrived(name, s, i, need=None):
+        when(need, desc[(name, s, i)].wait_recv)
+
+    def sends_done():
+        for copy, need in sent:
+            when(need, copy.wait_send)
+        sent.clear()
 
     local_count = [0]
 
-    def local(src, dst):
+    def local(src, dst, need=None):
         copy = pltpu.make_async_copy(src, dst, lsem.at[local_count[0]])
         local_count[0] += 1
-        copy.start()
+        when(need, copy.start)
         return copy
 
     peers = []
@@ -106,8 +120,10 @@
     for peer in peers:
         pl.semaphore_signal(barrier, inc=1, device_id=peer, device_id_type=MESH)
 
-    copies = [local(res_in, res), local(feat, xa.at[0:width, :]), local(binv_in, binv)]
+    copies = [local(res_in, res), local(feat, xa.at[0:width, :]), local(binv_in, binv),
+              local(co_in, co)]
     rcho[...] = jnp.zeros_like(rcho)
+    pbuf[...] = jnp.zeros_like(pbuf)
     diagonal = (lax.broadcasted_iota(jnp.int32, (PICK, PICK), 0)
                 == lax.broadcasted_iota(jnp.int32, (PICK, PICK), 1))
 
@@ -121,11 +137,10 @@
         return jnp.where(idxc[s] == position, 1.0, 0.0)
 
     def choose_res(s):
-        idxc[s] = chosen_at(s)
         pick = picks(s, 0, BLOCK).astype(BF16)
         res_hi = res[...].astype(BF16)
         res_lo = (res[...] - res_hi.astype(F32)).astype(BF16)
-        rcho[s, :, 0:outs] = dot_t(pick, res_hi) + dot_t(pick, res_lo)
+        rcho[s, 0:outs, :] = dot_t(res_hi, pick) + dot_t(res_lo, pick)
 
     def choose_feat(s):
         pick = picks(s, 0, BLOCK).astype(BF16)
@@ -135,6 +150,8 @@
         cho[s, :, tail_start:PAD_D] = with_norms(
             cho[s, :, tail_start:PAD_D].astype(F32), squares, tail_used + 3, tail_used).astype(BF16)
 
+    for s in range(2):
+        idxc[s] = chosen_at(s)
     copies[0].wait()
     choose_res(0)
     pl.semaphore_wait(barrier, len(peers))
@@ -144,10 +161,10 @@
     def r_rsx(s):
         for i in range(1, NX):
             xx = (x + i) % NX
-            send("r_rsx", s, i, rcho.at[s, pl.ds(pl.multiple_of(xx * 64, 64), 64), :],
+            send("r_rsx", s, i, rcho.at[s, pl.ds(pl.multiple_of(xx * 40, 8), 40), :],
                  rrx[s].at[x], dev(z, xx, y, k))
         waits[("r_rsx", s)] = local(
-            rcho.at[s, pl.ds(pl.multiple_of(x * 64, 64), 64), :], rrx[s].at[x])
+            rcho.at[s, pl.ds(pl.multiple_of(x * 40, 8), 40), :], rrx[s].at[x])
 
     def y_rsx(s):
         for i in range(NX):
@@ -170,11 +187,12 @@
         rsel[s] = rrx[s][owners[s] % NX]
         for i in range(NZ):
             zz = (z + i) % NZ
-            src = rsel.at[s, pl.ds(pl.multiple_of(zz * 8, 8), 8), :]
+            row = zz % 5
+            src = rsel.at[s, pl.ds(pl.multiple_of(row * 8, 8), 8), :]
             if i == 0:
-                waits[("r_rsz", s)] = local(src, rrz[s].at[z])
+                waits[("r_rsz", s)] = local(src, rrz[s].at[z], zz < 5)
             else:
-                send("r_rsz", s, i, src, rrz[s].at[z], dev(zz, x, y, k))
+                send("r_rsz", s, i, src, rrz[s].at[z], dev(zz, x, y, k), zz < 5)
 
     def y_rsz(s):
         for i in range(NX):
@@ -192,14 +210,18 @@
                 send("y_rsz", s, i, src, rz[s].at[z], dev(zz, x, y, k))
 
     def r_agz(s):
-        for i in range(1, NZ):
-            arrived("r_rsz", s, i)
-        waits[("r_rsz", s)].wait()
-        rch[s] = rrz[s][owners[s] // NX]
-        place = rbuf.at[s, pl.ds(pl.multiple_of(x * 64 + z * 8, 8), 8), :]
-        for i in range(1, NZ):
-            send("r_agz", s, i, rch.at[s], place, dev((z + i) % NZ, x, y, k))
-        waits[("r_agz", s)] = local(rch.at[s], place)
+        place = rbuf.at[s, pl.ds(pl.multiple_of(x * 40 + (z % 5) * 8, 8), 8), :]
+        for i in range(1, NZ):
+            arrived("r_rsz", s, i, z < 5)
+
+        @pl.when(z < 5)
+        def _():
+            waits[("r_rsz", s)].wait()
+            rch[s] = rrz[s][owners[s] // NX]
+
+        for i in range(1, NZ):
+            send("r_agz", s, i, rch.at[s], place, dev((z + i) % NZ, x, y, k), z < 5)
+        waits[("r_agz", s)] = local(rch.at[s], place, z < 5)
 
     def y_agz(s):
         for i in range(1, NZ):
@@ -214,9 +236,9 @@
 
     def r_agx(s):
         for i in range(1, NZ):
-            arrived("r_agz", s, i)
-        waits[("r_agz", s)].wait()
-        part = rbuf.at[s, pl.ds(pl.multiple_of(x * 64, 64), 64), :]
+            arrived("r_agz", s, i, (z - i + NZ) % NZ < 5)
+        when(z < 5, waits[("r_agz", s)].wait)
+        part = rbuf.at[s, pl.ds(pl.multiple_of(x * 40, 8), 40), :]
         for i in range(1, NX):
             send("r_agx", s, i, part, part, dev(z, (x + i) % NX, y, k))
 
@@ -291,8 +313,9 @@
                 arrived(kind + "_core", s, d * 4 + i)
 
     def partial_start(s, values):
-        pbuf[s] = jnp.dot(bg[s], values, precision=lax.Precision.HIGHEST,
-                          preferred_element_type=F32)
+        pbuf[s, :, 0:PAD_R] = lax.dot_general(
+            bg[s], values, (((1,), (1,)), ((), ())), precision=lax.Precision.HIGHEST,
+            preferred_element_type=F32)
         for i in range(NY * NK):
             cc = (c + i) % (NY * NK)
             src = pbuf.at[s, pl.ds(pl.multiple_of((cc // NK) * 16, 16), 16),
@@ -338,11 +361,11 @@
     choose_feat(0)
     r_rsz(0)
     y_rsx(0)
+    choose_feat(1)
+    y_rsx(1)
     choose_res(1)
-    choose_feat(1)
     r_agz(0)
     y_rsz(0)
-    y_rsx(1)
 
     @pl.loop(0, BLOCK // TILE)
     def _(t):
@@ -353,37 +376,33 @@
             xa[tail_start:PAD_D, at].astype(F32), squares, tail_used, tail_used + 3, 0).astype(BF16)
 
     r_agx(0)
+    y_rsz(1)
+    r_rsx(1)
     y_agz(0)
-    r_rsx(1)
     for i in range(1, NX):
         arrived("r_agx", 0, i)
     for i in range(1, NY * NK):
         arrived("b", 0, i)
     waits["b"].wait()
     partial_start(0, rbuf[0])
+    y_agz(1)
+    r_rsz(1)
     ag2_start("y", y_block, 0)
-    y_rsz(1)
     u_agz(0)
+    ag2_start("y", y_block, 1)
     ag3_start("y", y_block, 0)
-    r_rsz(1)
-    y_agz(1)
+    r_agz(1)
     ag2_start("u", u_block, 0)
+    ag3_start("y", y_block, 1)
     pass_start("y", y_block, 0)
-    r_agz(1)
     ag3_start("u", u_block, 0)
+    r_agx(1)
+    pass_start("y", y_block, 1)
+    pass_start("u", u_block, 0)
     core_start("y", y_block, 0)
-    ag2_start("y", y_block, 1)
-    pass_start("u", u_block, 0)
+    core_start("y", y_block, 1)
+    core_start("u", u_block, 0)
     core_end("y", 0)
-    r_agx(1)
-    gen(0, 0, 2)
-    core_start("u", u_block, 0)
-    ag3_start("y", y_block, 1)
-    gen(0, 2, 4)
-    pass_start("y", y_block, 1)
-    gen(0, 4, 6)
-    core_start("y", y_block, 1)
-    gen(0, 6, 8)
     core_end("y", 1)
 
     second = ybuf[1, c].reshape(PICK, PAD_D)
@@ -399,68 +418,73 @@
     for i in range(1, NX):
         arrived("r_agx", 1, i)
 
+    same = jnp.where(owners[0] == owners[1], 0.5, 0.0).astype(F32)
+    twice = jnp.where(idxc[1] == idxr[0:1, :], same, 0.0).astype(BF16)
     core_end("u", 0)
     turn(0)
-    moved = jnp.dot(k21[...], ubuf[0].reshape(BLOCK, PAD_C), preferred_element_type=F32)
-    same = jnp.where(owners[0] == owners[1], 0.5, 0.0).astype(F32)
-    twice = jnp.where(idxc[1] == idxr[0:1, :], same, 0.0).astype(BF16)
-    moved += jnp.dot(twice, ubuf[0, c].reshape(PICK, PAD_C), preferred_element_type=F32)
+    mine = pl.ds(pl.multiple_of(c * PICK, PICK), PICK)
+    moved = dot_t(ut[0, 0:PAD_R, :], k21[...])
+    moved += dot_t(ut[0, 0:PAD_R, mine], twice)
     partial_start(1, rbuf[1] - moved)
-    gen(1, 0, 2)
+
+    def product(s, t, from_res, from_co):
+        at = pl.ds(pl.multiple_of(t * 512, 512), 512)
+        change = jnp.dot(ut[s], kb[s, :, at], preferred_element_type=F32)
+        own = jnp.where(owners[s] == r, 1.0, 0.0).astype(F32)
+        put = (picks(s, t * 512, 512) * own).astype(BF16)
+        added = jnp.dot(ut[s, :, mine], put, preferred_element_type=F32)
+        new_res[:, at] = from_res[:, at] - (change + 0.5 * added)[:outs, :]
+        new_co[:, at] = from_co[:, at] + added[:outs, :]
+
+    gen(0, 0, 4)
     u_agz(1)
-    gen(1, 2, 4)
+    gen(0, 4, 8)
+    copies[3].wait()
     ag2_start("u", u_block, 1)
-    gen(1, 4, 6)
+
+    @pl.loop(0, 4)
+    def _(t):
+        product(0, t, res, co)
+
     ag3_start("u", u_block, 1)
-    gen(1, 6, 8)
+    gen(1, 0, 4)
     pass_start("u", u_block, 1)
+    gen(1, 4, 8)
     core_start("u", u_block, 1)
+    sends_done()
     core_end("u", 1)
-
     turn(1)
-    own = [jnp.where(owners[s] == r, 1.0, 0.0).astype(F32) for s in range(2)]
-    mine = [ut[s, :, pl.ds(pl.multiple_of(c * PICK, PICK), PICK)] for s in range(2)]
-
-    @pl.loop(0, BLOCK // 512)
+
+    @pl.loop(0, 4)
     def _(t):
-        at = pl.ds(pl.multiple_of(t * 512, 512), 512)
-        change = jnp.dot(ut[0], kb[0, :, at], preferred_element_type=F32)
-        change += jnp.dot(ut[1], kb[1, :, at], preferred_element_type=F32)
-        added = jnp.zeros((PAD_C, 512), F32)
-        for s in range(2):
-            put = (picks(s, t * 512, 512) * own[s]).astype(BF16)
-            added += jnp.dot(mine[s], put, preferred_element_type=F32)
-        chg[:, at] = (change + 0.5 * added)[:outs, :]
-        dco[:, at] = added[:outs, :]
-
-    for copy in desc.values():
-        copy.wait_send()
+        product(1, t, new_res, new_co)
 
 
 def per_device(features, residual, coeffs, block_inverse, block_index, owners):
     frames, width = features.shape
     outs = residual.shape[1]
     vmem = pl.BlockSpec(memory_space=pltpu.VMEM)
-    change, added = pl.pallas_call(
+    new_coeffs, new_residual = pl.pallas_call(
         functools.partial(body, width, outs),
         out_shape=(jax.ShapeDtypeStruct((outs, frames), F32),
                    jax.ShapeDtypeStruct((outs, frames), F32)),
-        in_specs=[pl.BlockSpec(memory_space=pltpu.SMEM)] + [pl.BlockSpec(memory_space=pl.ANY)] * 3 + [vmem],
+        in_specs=[pl.BlockSpec(memory_space=pltpu.SMEM)] + [pl.BlockSpec(memory_space=pl.ANY)] * 4 + [vmem],
         out_specs=(vmem, vmem),
         scratch_shapes=[
             pltpu.VMEM((2, PICK, 1), jnp.int32),
             pltpu.VMEM((outs, BLOCK), F32),
+            pltpu.VMEM((outs, BLOCK), F32),
             pltpu.VMEM((2, 8, BLOCK), F32),
             pltpu.VMEM((PAD_D, BLOCK), BF16),
             pltpu.VMEM((2, PICK, PAD_D), BF16),
-            pltpu.VMEM((2, PICK, PAD_C), F32),
-            pltpu.VMEM((NX, 64, PAD_C), F32),
-            pltpu.VMEM((NX, 64, PAD_C), F32),
-            pltpu.VMEM((2, 64, PAD_C), F32),
-            pltpu.VMEM((NZ, 8, PAD_C), F32),
-            pltpu.VMEM((NZ, 8, PAD_C), F32),
-            pltpu.VMEM((2, 8, PAD_C), F32),
-            pltpu.VMEM((2, PICK, PAD_C), F32),
+            pltpu.VMEM((2, PAD_R, PICK), F32),
+            pltpu.VMEM((NX, 40, PICK), F32),
+            pltpu.VMEM((NX, 40, PICK), F32),
+            pltpu.VMEM((2, 40, PICK), F32),
+            pltpu.VMEM((NZ, 8, PICK), F32),
+            pltpu.VMEM((NZ, 8, PICK), F32),
+            pltpu.VMEM((2, 8, PICK), F32),
+            pltpu.VMEM((2, PAD_R, PICK), F32),
             pltpu.VMEM((NX, NK, 64, 256), BF16),
             pltpu.VMEM((NX, NK, 64, 256), BF16),
             pltpu.VMEM((2, NK, 64, 256), BF16),
@@ -483,8 +507,8 @@
         compiler_params=pltpu.CompilerParams(
             collective_id=0, has_side_effects=True, vmem_limit_bytes=60 * 1024 * 1024),
         name="steps",
-    )(owners, features.T, residual.T, block_inverse, block_index)
-    return coeffs + added.T, residual - change.T
+    )(owners, features.T, residual.T, coeffs.T, block_inverse, block_index)
+    return new_coeffs.T, new_residual.T
 
 
 def solution(mesh):

time: 102 us -> 89.7 us (0.88)
  Pallas kernels: 97.4 us -> 85.4 us
  local copies, waits for them, and re-layouts: 0.01 us -> 3.58 us
  other arithmetic: 3.57 us -> 0 us
    pallas_call x1, Pallas kernels: 97.4 us -> 85.4 us  [per_device(): pl.pallas_call(functools.partial(body, width, outs), out_shape=(jax.Shape...]
    unnamed x4, local copies, waits for them, and re-layouts: 0.01 us -> 3.58 us
    sub x1 -> x0, other arithmetic: 3.57 us -> none  [per_device(): return (coeffs + added.T, residual - change.T)]
where the time goes in v3:
time: 89.7 us; the launch traced here: 89.6 us
  Pallas kernels  85.4 us (95%)
  local copies, waits for them, and re-layouts  3.58 us (4%)
    pallas_call x1, Pallas kernels, per_device(): pl.pallas_call(functools.partial(body, width, outs), out_shape=(jax.Shape...  85.4 us
    unnamed x4, local copies, waits for them, and re-layouts  3.58 us

profile of v3, /device:TPU:1, one launch (start us, length us, event | category | flops | bytes accessed | tf_op | source)
XLA Modules:
  0.0 89.6 jit_solution(6218408295202627266)
XLA Ops:
  0.6 85.4 %steps.1 = (f32[147,2048]{1,0:T(8,128)}, f32[147,2048]{1,0:T(8,128)}) custom-call(s32[2]{0:T(128)} %owners.1, bf16[440,2048]{1,0:T(8,128)(2,1)} %bitcast.5, f32[147,2048]{1,0:T(8,128)} %bitcast.6, f32[147,2048]{1,0:T(8,128)} %bitcast.7, f32[2,8,2048]{2,1,0:T(8,128)} %binv_in.1, s32[2,256]{1,0:T(2,128)} %idxr.1), custom_call_target="tpu_custom_call" | custom-call | tf_op jit(solution)/shard_map/steps/pallas_call | solution.py:467
  86.0 0.0 copy-start
  86.0 2.5 %copy.10 = f32[2048,147]{0,1:T(8,128)} copy(f32[2048,147]{0,1:T(8,128)} %bitcast.9) | data formatting | bytes 2408448
  88.6 0.0 copy-done
  88.6 1.0 %copy.11 = f32[2048,147]{0,1:T(8,128)} copy(f32[2048,147]{0,1:T(8,128)S(1)} %bitcast.8) | data formatting | bytes 2408448
Async XLA Ops:
  86.0 2.6 %copy-start = (f32[147,2048]{1,0:T(8,128)S(1)}, f32[147,2048]{1,0:T(8,128)}, u32[]{:S(2)}) copy-start(f32[147,2048]{1,0:T(8,128)} %get-tuple-element.5) | copy-start | bytes 3612676

commit v4 on v3

--- a/solution.py
+++ b/solution.py
@@ -55,9 +55,9 @@
     return jnp.where(lane == parts_at + 2, lo, out)
 
 
-def body(width, outs, owners, feat, res_in, co_in, binv_in, idxr, new_co, new_res,
+def body(width, outs, owners, feat, res_in, co_in, binv_in, idxr, co_out, res_out,
          idxc, res, co, binv, xa, cho, rcho, rrx0, rrx1, rsel, rrz0, rrz1, rch, rbuf, rx0, rx1, sel, rz0, rz1, ych,
-         ybuf, bg, pbuf, up, uch, ubuf, ut, kb, k21, ssem, rsem, lsem):
+         ybuf, bg, pbuf, up, uch, ubuf, ut, kb, k21, ssem, rsem, lsem, osem):
     rrx, rrz, rx, rz = (rrx0, rrx1), (rrz0, rrz1), (rx0, rx1), (rz0, rz1)
     r = lax.axis_index("rows")
     c = lax.axis_index("cols")
@@ -312,10 +312,11 @@
             for i in range(NY):
                 arrived(kind + "_core", s, d * 4 + i)
 
-    def partial_start(s, values):
-        pbuf[s, :, 0:PAD_R] = lax.dot_general(
-            bg[s], values, (((1,), (1,)), ((), ())), precision=lax.Precision.HIGHEST,
-            preferred_element_type=F32)
+    def inverse_times(s, values, dim):
+        return lax.dot_general(bg[s], values, (((1,), (dim,)), ((), ())),
+                               precision=lax.Precision.HIGHEST, preferred_element_type=F32)
+
+    def partial_start(s):
         for i in range(NY * NK):
             cc = (c + i) % (NY * NK)
             src = pbuf.at[s, pl.ds(pl.multiple_of((cc // NK) * 16, 16), 16),
@@ -384,10 +385,11 @@
     for i in range(1, NY * NK):
         arrived("b", 0, i)
     waits["b"].wait()
-    partial_start(0, rbuf[0])
+    pbuf[0, :, 0:PAD_R] = inverse_times(0, rbuf[0], 1)
+    partial_start(0)
+    ag2_start("y", y_block, 0)
     y_agz(1)
     r_rsz(1)
-    ag2_start("y", y_block, 0)
     u_agz(0)
     ag2_start("y", y_block, 1)
     ag3_start("y", y_block, 0)
@@ -420,21 +422,28 @@
 
     same = jnp.where(owners[0] == owners[1], 0.5, 0.0).astype(F32)
     twice = jnp.where(idxc[1] == idxr[0:1, :], same, 0.0).astype(BF16)
+    pbuf[1, :, 0:PAD_R] = inverse_times(1, rbuf[1], 1)
     core_end("u", 0)
+    moved = jnp.dot(k21[...], ubuf[0].reshape(BLOCK, PAD_C), preferred_element_type=F32)
+    moved += jnp.dot(twice, ubuf[0, c].reshape(PICK, PAD_C), preferred_element_type=F32)
+    pbuf[1] = pbuf[1] - inverse_times(1, moved, 0)
+    partial_start(1)
     turn(0)
     mine = pl.ds(pl.multiple_of(c * PICK, PICK), PICK)
-    moved = dot_t(ut[0, 0:PAD_R, :], k21[...])
-    moved += dot_t(ut[0, 0:PAD_R, mine], twice)
-    partial_start(1, rbuf[1] - moved)
-
-    def product(s, t, from_res, from_co):
+
+    def product(s, t):
         at = pl.ds(pl.multiple_of(t * 512, 512), 512)
-        change = jnp.dot(ut[s], kb[s, :, at], preferred_element_type=F32)
+        change = jnp.dot(ut[s, 0:PAD_R, :], kb[s, :, at], preferred_element_type=F32)
         own = jnp.where(owners[s] == r, 1.0, 0.0).astype(F32)
         put = (picks(s, t * 512, 512) * own).astype(BF16)
-        added = jnp.dot(ut[s, :, mine], put, preferred_element_type=F32)
-        new_res[:, at] = from_res[:, at] - (change + 0.5 * added)[:outs, :]
-        new_co[:, at] = from_co[:, at] + added[:outs, :]
+        added = jnp.dot(ut[s, 0:PAD_R, mine], put, preferred_element_type=F32)
+        res[:, at] = res[:, at] - (change + 0.5 * added)[:outs, :]
+        co[:, at] = co[:, at] + added[:outs, :]
+
+    def out_copies(t):
+        at = pl.ds(pl.multiple_of(t * 512, 512), 512)
+        return (pltpu.make_async_copy(res.at[:, at], res_out.at[:, at], osem.at[0, t]),
+                pltpu.make_async_copy(co.at[:, at], co_out.at[:, at], osem.at[1, t]))
 
     gen(0, 0, 4)
     u_agz(1)
@@ -444,8 +453,9 @@
 
     @pl.loop(0, 4)
     def _(t):
-        product(0, t, res, co)
-
+        product(0, t)
+
+    sends_done()
     ag3_start("u", u_block, 1)
     gen(1, 0, 4)
     pass_start("u", u_block, 1)
@@ -457,7 +467,18 @@
 
     @pl.loop(0, 4)
     def _(t):
-        product(1, t, new_res, new_co)
+        product(1, t)
+
+        @pl.when(t > 0)
+        def _():
+            for copy in out_copies(t - 1):
+                copy.start()
+
+    for copy in out_copies(3):
+        copy.start()
+    for t in range(4):
+        for copy in out_copies(t):
+            copy.wait()
 
 
 def per_device(features, residual, coeffs, block_inverse, block_index, owners):
@@ -469,7 +490,7 @@
         out_shape=(jax.ShapeDtypeStruct((outs, frames), F32),
                    jax.ShapeDtypeStruct((outs, frames), F32)),
         in_specs=[pl.BlockSpec(memory_space=pltpu.SMEM)] + [pl.BlockSpec(memory_space=pl.ANY)] * 4 + [vmem],
-        out_specs=(vmem, vmem),
+        out_specs=(pl.BlockSpec(memory_space=pl.ANY),) * 2,
         scratch_shapes=[
             pltpu.VMEM((2, PICK, 1), jnp.int32),
             pltpu.VMEM((outs, BLOCK), F32),
@@ -503,11 +524,13 @@
             pltpu.SemaphoreType.DMA((N_SEMS,)),
             pltpu.SemaphoreType.DMA((N_SEMS,)),
             pltpu.SemaphoreType.DMA((24,)),
+            pltpu.SemaphoreType.DMA((2, 4)),
         ],
         compiler_params=pltpu.CompilerParams(
-            collective_id=0, has_side_effects=True, vmem_limit_bytes=60 * 1024 * 1024),
+            collective_id=0, has_side_effects=True, vmem_limit_bytes=50 * 1024 * 1024),
         name="steps",
-    )(owners, features.T, residual.T, coeffs.T, block_inverse, block_index)
+    )(*[pltpu.with_memory_space_constraint(v, pltpu.HBM) for v in
+          (owners, features.T, residual.T, coeffs.T, block_inverse, block_index)])
     return new_coeffs.T, new_residual.T
 
 

time: 89.7 us -> 87.5 us (0.975)
  local copies, waits for them, and re-layouts: 3.58 us -> 2.07 us
    unnamed x4 -> x2, local copies, waits for them, and re-layouts: 3.58 us -> 2.07 us
where the time goes in v4:
time: 87.5 us; the launch traced here: 87.4 us
  Pallas kernels  84.7 us (97%)
  local copies, waits for them, and re-layouts  2.07 us (2%)
    pallas_call x1, Pallas kernels, per_device(): pl.pallas_call(functools.partial(body, width, outs), out_shape=(jax.Shape...  84.7 us
    unnamed x2, local copies, waits for them, and re-layouts  2.07 us

profile of v4, /device:TPU:1, one launch (start us, length us, event | category | flops | bytes accessed | tf_op | source)
XLA Modules:
  0.0 87.4 jit_solution(12319362357825142714)
XLA Ops:
  0.6 84.7 %steps.1 = (f32[147,2048]{1,0:T(8,128)S(1)}, f32[147,2048]{1,0:T(8,128)S(1)}) custom-call(s32[2]{0:T(128)} %owners.1, bf16[440,2048]{1,0:T(8,128)(2,1)} %bitcast.7, f32[147,2048]{1,0:T(8,128)} %bitcast.8, f32[147,2048]{1,0:T(8,128)} %bitcast.9, f32[2,8,2048]{2,1,0:T(8,128)} %binv_in.1, s32[2,256]{1,0:T(2,128)} %idxr.1), custom_call_target="tpu_custom_call" | custom-call | tf_op jit(solution)/shard_map/steps/pallas_call | solution.py:488
  85.3 1.0 %copy.10 = f32[2048,147]{0,1:T(8,128)} copy(f32[2048,147]{0,1:T(8,128)S(1)} %bitcast.6) | data formatting | bytes 2408448
  86.4 1.0 %copy.11 = f32[2048,147]{0,1:T(8,128)} copy(f32[2048,147]{0,1:T(8,128)S(1)} %bitcast.5) | data formatting | bytes 2408448

commit v5 on v4

--- a/solution.py
+++ b/solution.py
@@ -360,13 +360,13 @@
             send("b", 0, i, src, dst, (r, cc))
     copies[1].wait()
     choose_feat(0)
-    r_rsz(0)
     y_rsx(0)
     choose_feat(1)
     y_rsx(1)
+    r_rsz(0)
     choose_res(1)
+    y_rsz(0)
     r_agz(0)
-    y_rsz(0)
 
     @pl.loop(0, BLOCK // TILE)
     def _(t):
@@ -376,10 +376,12 @@
         xa[tail_start:PAD_D, at] = with_norms(
             xa[tail_start:PAD_D, at].astype(F32), squares, tail_used, tail_used + 3, 0).astype(BF16)
 
+    y_rsz(1)
+    y_agz(0)
     r_agx(0)
-    y_rsz(1)
     r_rsx(1)
-    y_agz(0)
+    y_agz(1)
+    ag2_start("y", y_block, 0)
     for i in range(1, NX):
         arrived("r_agx", 0, i)
     for i in range(1, NY * NK):
@@ -387,22 +389,20 @@
     waits["b"].wait()
     pbuf[0, :, 0:PAD_R] = inverse_times(0, rbuf[0], 1)
     partial_start(0)
-    ag2_start("y", y_block, 0)
-    y_agz(1)
     r_rsz(1)
+    ag2_start("y", y_block, 1)
     u_agz(0)
-    ag2_start("y", y_block, 1)
     ag3_start("y", y_block, 0)
     r_agz(1)
-    ag2_start("u", u_block, 0)
     ag3_start("y", y_block, 1)
     pass_start("y", y_block, 0)
+    ag2_start("u", u_block, 0)
+    core_start("y", y_block, 0)
+    pass_start("y", y_block, 1)
     ag3_start("u", u_block, 0)
     r_agx(1)
-    pass_start("y", y_block, 1)
+    core_start("y", y_block, 1)
     pass_start("u", u_block, 0)
-    core_start("y", y_block, 0)
-    core_start("y", y_block, 1)
     core_start("u", u_block, 0)
     core_end("y", 0)
     core_end("y", 1)
@@ -431,14 +431,19 @@
     turn(0)
     mine = pl.ds(pl.multiple_of(c * PICK, PICK), PICK)
 
-    def product(s, t):
+    def product(s, t, low, high):
         at = pl.ds(pl.multiple_of(t * 512, 512), 512)
-        change = jnp.dot(ut[s, 0:PAD_R, :], kb[s, :, at], preferred_element_type=F32)
+        change = jnp.dot(ut[s, low:high, :], kb[s, :, at], preferred_element_type=F32)
         own = jnp.where(owners[s] == r, 1.0, 0.0).astype(F32)
         put = (picks(s, t * 512, 512) * own).astype(BF16)
-        added = jnp.dot(ut[s, 0:PAD_R, mine], put, preferred_element_type=F32)
-        res[:, at] = res[:, at] - (change + 0.5 * added)[:outs, :]
-        co[:, at] = co[:, at] + added[:outs, :]
+        added = jnp.dot(ut[s, low:high, mine], put, preferred_element_type=F32)
+        top = min(high, outs)
+        res[low:top, at] = res[low:top, at] - (change + 0.5 * added)[:top - low, :]
+        co[low:top, at] = co[low:top, at] + added[:top - low, :]
+
+    def turn_half(h):
+        ut[1, h * 128:(h + 1) * 128, :] = jnp.transpose(
+            ubuf[1, :, :, :, :, h * 128:(h + 1) * 128].reshape(BLOCK, 128))
 
     def out_copies(t):
         at = pl.ds(pl.multiple_of(t * 512, 512), 512)
@@ -453,29 +458,42 @@
 
     @pl.loop(0, 4)
     def _(t):
-        product(0, t)
+        product(0, t, 0, PAD_R)
 
     sends_done()
     ag3_start("u", u_block, 1)
     gen(1, 0, 4)
     pass_start("u", u_block, 1)
     gen(1, 4, 8)
+    sends_done()
     core_start("u", u_block, 1)
-    sends_done()
+    for h, (low, high) in enumerate(((0, 128), (128, PAD_R))):
+        @pl.when(k == h)
+        def _():
+            turn_half(h)
+
+            @pl.loop(0, 4)
+            def _(t):
+                product(1, t, low, high)
+
     core_end("u", 1)
-    turn(1)
-
-    @pl.loop(0, 4)
-    def _(t):
-        product(1, t)
-
-        @pl.when(t > 0)
+    for h, (low, high) in enumerate(((0, 128), (128, PAD_R))):
+        @pl.when(k == 1 - h)
         def _():
-            for copy in out_copies(t - 1):
-                copy.start()
+            turn_half(h)
+
+            @pl.loop(0, 4)
+            def _(t):
+                product(1, t, low, high)
+
+                @pl.when(t > 0)
+                def _():
+                    for copy in out_copies(t - 1):
+                        copy.start()
 
     for copy in out_copies(3):
         copy.start()
+    sends_done()
     for t in range(4):
         for copy in out_copies(t):
             copy.wait()

time: 87.5 us -> 87.5 us (level)
  no operation moved by 1% of the time
where the time goes in v5:
time: 87.5 us; the launch traced here: 87.4 us
  Pallas kernels  84.7 us (97%)
  local copies, waits for them, and re-layouts  2.07 us (2%)
    pallas_call x1, Pallas kernels, per_device(): pl.pallas_call(functools.partial(body, width, outs), out_shape=(jax.Shape...  84.7 us
    unnamed x2, local copies, waits for them, and re-layouts  2.07 us

profile of v5, /device:TPU:1, one launch (start us, length us, event | category | flops | bytes accessed | tf_op | source)
XLA Modules:
  0.0 87.4 jit_solution(3138542649197806375)
XLA Ops:
  0.6 84.7 %steps.1 = (f32[147,2048]{1,0:T(8,128)S(1)}, f32[147,2048]{1,0:T(8,128)S(1)}) custom-call(s32[2]{0:T(128)} %owners.1, bf16[440,2048]{1,0:T(8,128)(2,1)} %bitcast.7, f32[147,2048]{1,0:T(8,128)} %bitcast.8, f32[147,2048]{1,0:T(8,128)} %bitcast.9, f32[2,8,2048]{2,1,0:T(8,128)} %binv_in.1, s32[2,256]{1,0:T(2,128)} %idxr.1), custom_call_target="tpu_custom_call" | custom-call | tf_op jit(solution)/shard_map/steps/pallas_call | solution.py:506
  85.3 1.0 %copy.10 = f32[2048,147]{0,1:T(8,128)} copy(f32[2048,147]{0,1:T(8,128)S(1)} %bitcast.6) | data formatting | bytes 2408448
  86.4 1.0 %copy.11 = f32[2048,147]{0,1:T(8,128)} copy(f32[2048,147]{0,1:T(8,128)S(1)} %bitcast.5) | data formatting | bytes 2408448

commit v6 on v5

--- a/solution.py
+++ b/solution.py
@@ -379,9 +379,9 @@
     y_rsz(1)
     y_agz(0)
     r_agx(0)
-    r_rsx(1)
     y_agz(1)
     ag2_start("y", y_block, 0)
+    r_rsx(1)
     for i in range(1, NX):
         arrived("r_agx", 0, i)
     for i in range(1, NY * NK):
@@ -389,14 +389,14 @@
     waits["b"].wait()
     pbuf[0, :, 0:PAD_R] = inverse_times(0, rbuf[0], 1)
     partial_start(0)
-    r_rsz(1)
     ag2_start("y", y_block, 1)
     u_agz(0)
+    r_rsz(1)
     ag3_start("y", y_block, 0)
-    r_agz(1)
     ag3_start("y", y_block, 1)
     pass_start("y", y_block, 0)
     ag2_start("u", u_block, 0)
+    r_agz(1)
     core_start("y", y_block, 0)
     pass_start("y", y_block, 1)
     ag3_start("u", u_block, 0)
@@ -404,6 +404,9 @@
     core_start("y", y_block, 1)
     pass_start("u", u_block, 0)
     core_start("u", u_block, 0)
+    for i in range(1, NX):
+        arrived("r_agx", 1, i)
+    pbuf[1, :, 0:PAD_R] = inverse_times(1, rbuf[1], 1)
     core_end("y", 0)
     core_end("y", 1)
 
@@ -417,12 +420,8 @@
     for j in range(4):
         inner = dot_t(second, ybuf[0, 2 * j:2 * j + 2].reshape(512, PAD_D))
         k21[:, j * 512:(j + 1) * 512] = jnp.exp2(inner * scale).astype(BF16)
-    for i in range(1, NX):
-        arrived("r_agx", 1, i)
-
     same = jnp.where(owners[0] == owners[1], 0.5, 0.0).astype(F32)
     twice = jnp.where(idxc[1] == idxr[0:1, :], same, 0.0).astype(BF16)
-    pbuf[1, :, 0:PAD_R] = inverse_times(1, rbuf[1], 1)
     core_end("u", 0)
     moved = jnp.dot(k21[...], ubuf[0].reshape(BLOCK, PAD_C), preferred_element_type=F32)
     moved += jnp.dot(twice, ubuf[0, c].reshape(PICK, PAD_C), preferred_element_type=F32)
@@ -453,6 +452,7 @@
     gen(0, 0, 4)
     u_agz(1)
     gen(0, 4, 8)
+    sends_done()
     copies[3].wait()
     ag2_start("u", u_block, 1)
 
@@ -460,7 +460,6 @@
     def _(t):
         product(0, t, 0, PAD_R)
 
-    sends_done()
     ag3_start("u", u_block, 1)
     gen(1, 0, 4)
     pass_start("u", u_block, 1)

time: 87.5 us -> 87.3 us (level)
  no operation moved by 1% of the time
where the time goes in v6:
time: 87.3 us; the launch traced here: 86.7 us
  Pallas kernels  84 us (96%)
  local copies, waits for them, and re-layouts  2.07 us (2%)
    pallas_call x1, Pallas kernels, per_device(): pl.pallas_call(functools.partial(body, width, outs), out_shape=(jax.Shape...  84 us
    unnamed x2, local copies, waits for them, and re-layouts  2.07 us

profile of v6, /device:TPU:1, one launch (start us, length us, event | category | flops | bytes accessed | tf_op | source)
XLA Modules:
  0.0 86.7 jit_solution(11450007019119592932)
XLA Ops:
  0.6 84.0 %steps.1 = (f32[147,2048]{1,0:T(8,128)S(1)}, f32[147,2048]{1,0:T(8,128)S(1)}) custom-call(s32[2]{0:T(128)} %owners.1, bf16[440,2048]{1,0:T(8,128)(2,1)} %bitcast.7, f32[147,2048]{1,0:T(8,128)} %bitcast.8, f32[147,2048]{1,0:T(8,128)} %bitcast.9, f32[2,8,2048]{2,1,0:T(8,128)} %binv_in.1, s32[2,256]{1,0:T(2,128)} %idxr.1), custom_call_target="tpu_custom_call" | custom-call | tf_op jit(solution)/shard_map/steps/pallas_call | solution.py:505
  84.7 1.0 %copy.10 = f32[2048,147]{0,1:T(8,128)} copy(f32[2048,147]{0,1:T(8,128)S(1)} %bitcast.6) | data formatting | bytes 2408448
  85.7 1.0 %copy.11 = f32[2048,147]{0,1:T(8,128)} copy(f32[2048,147]{0,1:T(8,128)S(1)} %bitcast.5) | data formatting | bytes 2408448

commit v7 on v6

--- a/solution.py
+++ b/solution.py
@@ -239,8 +239,15 @@
             arrived("r_agz", s, i, (z - i + NZ) % NZ < 5)
         when(z < 5, waits[("r_agz", s)].wait)
         part = rbuf.at[s, pl.ds(pl.multiple_of(x * 40, 8), 40), :]
-        for i in range(1, NX):
+        for i in (1, 3):
             send("r_agx", s, i, part, part, dev(z, (x + i) % NX, y, k))
+
+    def r_agx_pass(s):
+        for i, slot, first, rows in ((1, 2, 0, 24), (3, 0, 24, 16)):
+            arrived("r_agx", s, i)
+            start = ((x - i + NX) % NX) * 40 + first
+            part = rbuf.at[s, pl.ds(pl.multiple_of(start, 8), rows), :]
+            send("r_agx", s, slot, part, part, dev(z, (x + i) % NX, y, k))
 
     g = (1 - k) * x + k * y
     q = (1 - k) * y + k * x
@@ -379,10 +386,11 @@
     y_rsz(1)
     y_agz(0)
     r_agx(0)
+    r_agx_pass(0)
     y_agz(1)
     ag2_start("y", y_block, 0)
     r_rsx(1)
-    for i in range(1, NX):
+    for i in (0, 2):
         arrived("r_agx", 0, i)
     for i in range(1, NY * NK):
         arrived("b", 0, i)
@@ -401,10 +409,11 @@
     pass_start("y", y_block, 1)
     ag3_start("u", u_block, 0)
     r_agx(1)
+    r_agx_pass(1)
     core_start("y", y_block, 1)
     pass_start("u", u_block, 0)
     core_start("u", u_block, 0)
-    for i in range(1, NX):
+    for i in (0, 2):
         arrived("r_agx", 1, i)
     pbuf[1, :, 0:PAD_R] = inverse_times(1, rbuf[1], 1)
     core_end("y", 0)

time: 87.3 us -> 89.8 us (1.029)
  Pallas kernels: 84 us -> 86.6 us
    pallas_call x1, Pallas kernels: 84 us -> 86.6 us  [per_device(): pl.pallas_call(functools.partial(body, width, outs), out_shape=(jax.Shape...]
where the time goes in v7:
time: 89.8 us; the launch traced here: 89.4 us
  Pallas kernels  86.6 us (96%)
  local copies, waits for them, and re-layouts  2.07 us (2%)
    pallas_call x1, Pallas kernels, per_device(): pl.pallas_call(functools.partial(body, width, outs), out_shape=(jax.Shape...  86.6 us
    unnamed x2, local copies, waits for them, and re-layouts  2.07 us

profile of v7, /device:TPU:1, one launch (start us, length us, event | category | flops | bytes accessed | tf_op | source)
XLA Modules:
  0.0 89.4 jit_solution(649985610059599391)
XLA Ops:
  0.6 86.6 %steps.1 = (f32[147,2048]{1,0:T(8,128)S(1)}, f32[147,2048]{1,0:T(8,128)S(1)}) custom-call(s32[2]{0:T(128)} %owners.1, bf16[440,2048]{1,0:T(8,128)(2,1)} %bitcast.7, f32[147,2048]{1,0:T(8,128)} %bitcast.8, f32[147,2048]{1,0:T(8,128)} %bitcast.9, f32[2,8,2048]{2,1,0:T(8,128)} %binv_in.1, s32[2,256]{1,0:T(2,128)} %idxr.1), custom_call_target="tpu_custom_call" | custom-call | tf_op jit(solution)/shard_map/steps/pallas_call | solution.py:514
  87.3 1.0 %copy.10 = f32[2048,147]{0,1:T(8,128)} copy(f32[2048,147]{0,1:T(8,128)S(1)} %bitcast.6) | data formatting | bytes 2408448
  88.3 1.0 %copy.11 = f32[2048,147]{0,1:T(8,128)} copy(f32[2048,147]{0,1:T(8,128)S(1)} %bitcast.5) | data formatting | bytes 2408448
